TPU v7x, 32 devices: a whole 2x2x4 slice. The times are simulated.
32 devices in a mesh: grp: 4 (over x, core), dev: 8 (over z, y).
Axes of the slice: x: 2, y: 2, z: 4, core: 2. Of those that a mesh axis runs over, the one named last changes fastest.
Arguments:
- tracer: float32 [96, 131072], P(None, ('grp', 'dev')), may hold values from 0.05 to 2
- tile_rows: int32 [5120], P(('grp', 'dev')), may hold values from 0 to 1023, as said below
- tile_cols: int32 [5120], P(('grp', 'dev')), may hold values from 0 to 1023, as said below
- tile_values: bfloat16 [5120, 128, 128], P(('grp', 'dev')), may hold values from -0.25 to 0.25
- level_counts: int32 [4096], P(('grp', 'dev')), may hold values from 1 to 32, as said below
- column_owner: int32 [4096], P(('grp', 'dev')), may hold values from 0 to 7, as said below
- half_saturation: float32 [16], replicated, may hold values from 0.1 to 1
- growth_rate: float32 [64], replicated, may hold values from 0.2 to 2
- uptake: float32 [64, 16], replicated, may hold values from 0 to 0.125
- graze_preference: float32 [64, 64], replicated, may hold values from 0 to 0.03125
- graze_maximum: float32 [64], replicated, may hold values from 0.2 to 2
Outputs:
- updated: float32 [96, 131072], P(None, ('grp', 'dev'))
- production: float32 [4096], P(('grp', 'dev'))
Inputs may be any that keep to these rules, and one draw needn't show every extreme that they name: `tile_rows`: each device holds 160 tiles; taken device after device along dev, the tiles of a group run in increasing row block. Device d of the whole chain of devices owns row blocks d * 32 to d * 32 + 31; its tiles have row blocks of its own or, among its first 20 tiles only, of the device before it in its group. Device 1 of every group holds exactly 20 tiles of device 0's row blocks. `tile_cols`: A tile's column block lies within 16 blocks of its row block, and within the blocks owned by the device that holds the tile and its two neighbours in the chain. `level_counts`: every device's first column has 32 wet levels, its second one 1. `column_owner`: every device sends exactly 16 of its columns to each device of its group.
All inputs are finite; a program needn't handle non-finite values.
Results may differ from a plain program's by a relative error of at most 0.0018.
Values may be sent and summed in bfloat16 or wider, within the bound.
No kernel may reach another device: no remote copies, remote signals or barrier semaphores. Data moves between devices by JAX's collectives and lax.ppermute only.
A program may use at most 64 MiB of HBM per device.

v0:
```python
import jax
import jax.numpy as jnp
from jax import lax
from jax.sharding import PartitionSpec as P

NUT = 16
PLK = 64
LEV = 32


highest = lax.Precision.HIGHEST
WATER_DECAY = 0.03
SHADE_DECAY = 0.05
EFFICIENCY = 0.3
MORTALITY = 0.1
REMINERAL = 0.2
TIMESTEP = 0.5


def with_halo(x, sides, width):
    for axis, dim in sides:
        count, length = (lax.axis_size(axis), x.shape[dim])
        up = [(i, (i + 1) % count) for i in range(count - 1)]
        down = [(j, i) for i, j in up]
        last = lax.slice_in_dim(x, length - width, length, axis=dim)
        initial = lax.slice_in_dim(x, 0, width, axis=dim)
        before = lax.ppermute(last, axis, up)
        after = lax.ppermute(initial, axis, down)
        x = jnp.concatenate([before, x, after], axis=dim)
    return x


def from_behind(value, axis, steps):
    count = lax.axis_size(axis)
    initial, last = (max(0, -steps), min(count, count - steps))
    return lax.ppermute(value, axis, [(source, source + steps) for source in range(initial, last)])


def ecosystem(cells, levels, half_saturation, growth_rate, uptake, graze_preference, graze_maximum):
    column_count = levels.shape[0]
    depth_index = lax.broadcasted_iota(jnp.int32, (column_count, LEV), 1).astype(jnp.float32)
    wet_mask = (depth_index < levels[:, None]).astype(jnp.float32).reshape(1, column_count * LEV)
    nutrient = cells[:NUT]
    plankton = cells[NUT : NUT + PLK]
    detritus = cells[NUT + PLK :]
    chlorophyll = (jnp.sum(plankton, axis=0, keepdims=True) / PLK * wet_mask).reshape(
        column_count, LEV
    )
    above_mask = (
        lax.broadcasted_iota(jnp.int32, (LEV, LEV), 0)
        < lax.broadcasted_iota(jnp.int32, (LEV, LEV), 1)
    ).astype(jnp.float32)
    shading = jnp.dot(chlorophyll, above_mask, precision=highest).reshape(1, column_count * LEV)
    sunlight = jnp.exp(
        -WATER_DECAY * depth_index.reshape(1, column_count * LEV) - SHADE_DECAY * shading
    )
    monod_term = nutrient / (nutrient + half_saturation[:, None])
    limitation = jnp.dot(uptake, monod_term, precision=highest)
    capacity = growth_rate[:, None] * sunlight * plankton
    growth = capacity * limitation
    food_sum = jnp.dot(graze_preference, plankton, precision=highest)
    graze_rate = graze_maximum[:, None] * plankton / (1.0 + food_sum)
    grazed = plankton * jnp.dot(graze_preference.T, graze_rate, precision=highest)
    eaten_total = graze_rate * food_sum
    d_plankton = growth - grazed + EFFICIENCY * eaten_total - MORTALITY * plankton
    d_nutrient = -monod_term * jnp.dot(uptake.T, capacity, precision=highest) + REMINERAL * detritus
    waste_flux = ((1.0 - EFFICIENCY) * eaten_total + MORTALITY * plankton).reshape(
        NUT, PLK // NUT, column_count * LEV
    )
    d_detritus = jnp.sum(waste_flux, axis=1) - REMINERAL * detritus
    source = jnp.concatenate([d_nutrient, d_plankton, d_detritus], axis=0) * wet_mask
    column_sum = jnp.sum(
        (jnp.sum(growth, axis=0) / PLK * wet_mask[0]).reshape(column_count, LEV), axis=1
    )
    return (source, column_sum)


def per_device(
    tracer,
    tile_rows,
    tile_cols,
    tile_values,
    level_counts,
    column_owner,
    half_saturation,
    growth_rate,
    uptake,
    graze_preference,
    graze_maximum,
):
    channels, cell_count = tracer.shape
    tile_total = tile_rows.shape[0]
    block_size = tile_values.shape[1]
    block_count = cell_count // block_size
    position = lax.axis_index("grp") * lax.axis_size("dev") + lax.axis_index("dev")
    coarse = tracer.astype(jnp.bfloat16)
    extended = with_halo(coarse, ((("grp", "dev"), 1),), cell_count)
    ext_blocks = extended.reshape(channels, 3 * block_count, block_size)
    window_start = (position - 1) * block_count
    spill_size = tile_total // 8
    incoming_tiles = from_behind(
        (tile_values[:spill_size], tile_rows[:spill_size], tile_cols[:spill_size]), "dev", -1
    )
    all_data = jnp.concatenate([tile_values, incoming_tiles[0]], axis=0)
    all_rows = jnp.concatenate([tile_rows, incoming_tiles[1]], axis=0)
    all_cols = jnp.concatenate([tile_cols, incoming_tiles[2]], axis=0)
    local_block = jnp.clip(all_cols - window_start, 0, 3 * block_count - 1)
    picked = jnp.take(ext_blocks, local_block, axis=1)
    contrib = jnp.einsum("ctb,tab->tca", picked, all_data, preferred_element_type=jnp.float32)
    row_slot = all_rows - position * block_count
    onehot = (row_slot[:, None] == jnp.arange(block_count)[None, :]).astype(jnp.float32)
    transport = jnp.einsum("tw,tca->cwa", onehot, contrib, precision=highest).reshape(
        channels, cell_count
    )
    send_order = jnp.argsort(column_owner, stable=True)
    source, local_sums = ecosystem(
        tracer,
        level_counts.astype(jnp.float32),
        half_saturation,
        growth_rate,
        uptake,
        graze_preference,
        graze_maximum,
    )
    production = lax.all_to_all(
        local_sums[send_order], "dev", split_axis=0, concat_axis=0, tiled=True
    )
    updated = tracer + transport + TIMESTEP * source
    return (updated, production)


def solution(mesh):
    return jax.shard_map(
        per_device,
        mesh=mesh,
        in_specs=(
            P(None, ("grp", "dev")),
            P(("grp", "dev")),
            P(("grp", "dev")),
            P(("grp", "dev"), None, None),
            P(("grp", "dev")),
            P(("grp", "dev")),
            P(),
            P(),
            P(),
            P(),
            P(),
        ),
        out_specs=(P(None, ("grp", "dev")), P(("grp", "dev"))),
        check_vma=False,
    )
```

profile of v0, /device:TPU:2, one launch (start us, length us, event | category | flops | bytes accessed | tf_op | source)
XLA Modules:
  0.0 84.3 jit_solution(18431979715139781458)
XLA Ops:
  0.6 0.0 copy-start
  0.6 0.0 copy-start.1
  0.7 1.6 %convert_element_type.29 = bf16[96,4096]{1,0:T(8,128)(2,1)S(1)} convert(f32[96,4096]{1,0:T(8,128)} %param.11) | non-fusion elementwise | flops 393216 | bytes 2359296 | tf_op jit(solution)/shard_map/convert_element_type | solution.py:96
  2.3 3.4 %collective-permute-start.1 = (bf16[96,4096]{1,0:T(8,128)(2,1)S(1)}, bf16[96,4096]{1,0:T(8,128)(2,1)}, u32[]{:S(2)}, u32[]{:S(2)}) collective-permute-start(bf16[96,4096]{1,0:T(8,128)(2,1)S(1)} %convert_element_type.29), channel_id=1, source_target_pairs={{0,1},{1,2},{2,3},{3,4},{4,5},{5,6},{6,7},{7,8},{8,9},{9,10},{10,1... | collective-permute-start | bytes 2359304 | tf_op jit(solution)/shard_map/ppermute | solution.py:27
  5.7 5.7 %collective-permute-start.2 = (bf16[96,4096]{1,0:T(8,128)(2,1)S(1)}, bf16[96,4096]{1,0:T(8,128)(2,1)}, u32[]{:S(2)}, u32[]{:S(2)}) collective-permute-start(bf16[96,4096]{1,0:T(8,128)(2,1)S(1)} %convert_element_type.29), channel_id=1, source_target_pairs={{1,0},{2,1},{3,2},{4,3},{5,4},{6,5},{7,6},{8,7},{9,8},{10,9},{11,1... | collective-permute-start | bytes 2359304 | tf_op jit(solution)/shard_map/ppermute | solution.py:28
  11.5 1.3 %collective-permute-start = (s32[20]{0:T(128)S(1)}, s32[20]{0:T(128)S(1)}, u32[]{:S(2)}, u32[]{:S(2)}) collective-permute-start(s32[20]{0:T(128)S(1)} %slice.18), channel_id=1, source_target_pairs={{1,0},{2,1},{3,2},{4,3},{5,4},{6,5},{7,6},{9,8},{10,9},{11,10},{12... | collective-permute-start | bytes 248 | tf_op jit(solution)/shard_map/ppermute | solution.py:36
  12.8 2.0 %slice.19 = bf16[20,128,128]{2,1,0:T(8,128)(2,1)} slice(bf16[160,128,128]{2,1,0:T(8,128)(2,1)} %param.14), slice={[0:20], [0:128], [0:128]} | slice | bytes 1310720 | tf_op jit(solution)/shard_map/slice | solution.py:102
  14.8 1.3 %collective-permute-start.3 = (bf16[20,128,128]{2,1,0:T(8,128)(2,1)}, bf16[20,128,128]{2,1,0:T(8,128)(2,1)}, u32[]{:S(2)}, u32[]{:S(2)}) collective-permute-start(bf16[20,128,128]{2,1,0:T(8,128)(2,1)} %slice.19), channel_id=1, source_target_pairs={{1,0},{2,1},{3,2},{4,3},{5,4},{6,5},{7,6},{9,8},{10,9},{11,10},{12... | collective-permute-start | bytes 1966088 | tf_op jit(solution)/shard_map/ppermute | solution.py:36
  16.1 1.3 %collective-permute-start.4 = (s32[20]{0:T(128)S(1)}, s32[20]{0:T(128)S(1)}, u32[]{:S(2)}, u32[]{:S(2)}) collective-permute-start(s32[20]{0:T(128)S(1)} %slice.20), channel_id=1, source_target_pairs={{1,0},{2,1},{3,2},{4,3},{5,4},{6,5},{7,6},{9,8},{10,9},{11,10},{12... | collective-permute-start | bytes 248 | tf_op jit(solution)/shard_map/ppermute | solution.py:36
  17.5 0.0 copy-start.8
  17.5 0.0 copy-start.7
  17.5 0.0 copy-start.11
  17.5 0.0 copy-start.12
  17.5 2.6 %slice_reduce_fusion = (f32[4096]{0:T(1024)S(1)}, f32[64,4096]{1,0:T(8,128)}, f32[64,4096]{1,0:T(8,128)}) fusion(f32[96,4096]{1,0:T(8,128)S(1)} %copy-done.1, f32[64]{0:T(128)S(1)} %copy-done.10, f32[64,64]{1,0:T(8,128)S(1)} %copy-done), kind=kOutput, calls=%fused_computation.39 | convolution fusion | flops 203419648 | bytes 4243968 | tf_op jit(solution)/shard_map/dot_general | solution.py:61
  20.1 0.1 div.23
  20.2 0.3 fusion.20
  20.5 0.1 copy.20
  20.6 0.1 exp.12
  20.7 0.0 copy-done.7
  20.7 2.2 %fusion.44 = (f32[4096]{0:T(1024)S(1)}, f32[64,4096]{1,0:T(8,128)}) fusion(f32[64,16]{0,1:T(8,128)S(1)} %copy-done.7, f32[96,4096]{1,0:T(8,128)S(1)} %copy-done.1, f32[16]{0:T(128)S(1)} %copy-done.11, f32[4096]{0:T(1024)S(1)} %exp.12, f32[64]{0:T(128)S(1)} %copy-done.12), kind=kOutput, calls=%fused_computation.77 | convolution fusion | flops 51507200 | bytes 2401280 | tf_op jit(solution)/shard_map/dot_general | solution.py:58
  22.9 0.1 div.26
  23.0 0.2 fusion.31
  23.2 2.5 %sort.17 = (s32[128]{0:T(128)}, s32[128]{0:T(128)S(1)}) sort(s32[128]{0:T(128)S(1)} %copy-done.9, s32[128]{0:T(128)S(1)} %iota.33), dimensions={0}, to_apply=%region_4.5 | sort | flops 896 | bytes 2048 | tf_op jit(solution)/shard_map/jit(argsort)/sort | solution.py:115
  25.7 1.2 %gather_fusion.1 = f32[128]{0:T(128)S(1)} fusion(f32[128]{0:T(128)S(1)} %fusion.31, s32[1024]{0:T(1024)S(1)} %pad_clamp_fusion), kind=kCustom, calls=%fused_computation.1 | custom fusion | bytes 1536 | tf_op jit(solution)/shard_map/gather | solution.py:126
  27.0 0.7 all_to_all.8
  27.6 8.1 %all-to-all-start = ((f32[8,16,1]{1,2,0:T(1,128)}), f32[8,16,1]{1,2,0:T(1,128)S(1)}, u32[]{:S(2)}, u32[]{:S(2)}) async-start(f32[8,16,1]{1,2,0:T(1,128)} %bitcast.9), calls=%async_computation | async-start | bytes 8192 | tf_op jit(solution)/shard_map/all_to_all | solution.py:125
  35.7 1.5 %reshape.149 = f32[16,4,4096]{2,1,0:T(4,128)S(1)} reshape(f32[64,4096]{1,0:T(8,128)} %get-tuple-element.5) | data formatting | bytes 2097152 | tf_op jit(solution)/shard_map/reshape | solution.py:67
  37.3 1.4 %reduce_sum.37 = f32[16,4096]{1,0:T(8,128)} reduce(f32[16,4,4096]{2,1,0:T(4,128)S(1)} %reshape.149, f32[]{:T(128)} %constant.17.clone.1), dimensions={1}, to_apply=%region_1.2 | reduce | flops 196608 | bytes 1310724 | tf_op jit(solution)/shard_map/reduce_sum | solution.py:70
  38.6 1.0 %fusion.30 = f32[16,4096]{1,0:T(8,128)S(1)} fusion(f32[16,4096]{1,0:T(8,128)} %reduce_sum.37, f32[96,4096]{1,0:T(8,128)S(1)} %copy-done.1), kind=kLoop, calls=%fused_computation.46 | loop fusion | flops 131072 | bytes 786432 | tf_op jit(solution)/shard_map/sub | solution.py:70
  39.6 4.5 %fusion.10 = f32[64,4096]{1,0:T(8,128)} fusion(f32[64,4096]{1,0:T(8,128)} %get-tuple-element.8, f32[64,64]{1,0:T(8,128)S(1)} %copy-done, f32[64,4096]{1,0:T(8,128)} %get-tuple-element.6, f32[96,4096]{1,0:T(8,128)S(1)} %copy-done.1, f32[64]{0:T(128)S(1)} %copy-done.10), kind=kOutput, calls=%fused_computation.14 | convolution fusion | flops 204734464 | bytes 6325248 | tf_op jit(solution)/shard_map/dot_general | solution.py:63
  44.1 1.5 %fusion.12 = f32[16,4096]{1,0:T(8,128)} fusion(f32[64,16]{0,1:T(8,128)S(1)} %copy-done.7, f32[96,4096]{1,0:T(8,128)S(1)} %copy-done.1, f32[4096]{0:T(1024)S(1)} %exp.12, f32[64]{0:T(128)S(1)} %copy-done.12, f32[16]{0:T(128)S(1)} %copy-done.11), kind=kOutput, calls=%fused_computation.17 | convolution fusion | flops 51249152 | bytes 1855808 | tf_op jit(solution)/shard_map/dot_general | solution.py:66
  45.6 0.1 compare_convert_fusion
  45.7 0.1 reshape.150
  45.8 0.1 compare_select_fusion.3
  45.9 11.8 %collective-permute-done.4 = s32[20]{0:T(128)S(1)} collective-permute-done((s32[20]{0:T(128)S(1)}, s32[20]{0:T(128)S(1)}, u32[]{:S(2)}, u32[]{:S(2)}) %collective-permute-start.4) | collective-permute-done | bytes 112 | tf_op jit(solution)/shard_map/ppermute | solution.py:36
  57.7 0.1 add_subtract_fusion.2
  57.8 0.1 compare_and_fusion
  57.9 0.0 all-to-all-done
  57.9 0.5 broadcast.137
  58.4 0.7 reduce.3
  59.0 0.6 all_to_all.10
  59.6 1.8 %copy_bitcast_fusion = bf16[96,96,128]{2,0,1:T(8,128)(2,1)S(1)} fusion(bf16[96,4096]{1,0:T(8,128)(2,1)} %collective-permute-done.2, bf16[96,4096]{1,0:T(8,128)(2,1)S(1)} %convert_element_type.29, bf16[96,4096]{1,0:T(8,128)(2,1)} %collective-permute-done.1), kind=kLoop, calls=%fused_computation.21 | loop fusion | flops 7077888 | bytes 4718592 | tf_op jit(solution)/shard_map/reshape | solution.py:98
  61.4 3.3 %gather_fusion = bf16[180,96,128]{2,1,0:T(8,128)(2,1)} fusion(bf16[96,96,128]{2,0,1:T(8,128)(2,1)S(1)} %copy_bitcast_fusion, s32[1024]{0:T(1024)S(1)} %pad_clamp_fusion.1), kind=kCustom, calls=%fused_computation | custom fusion | bytes 8848080 | tf_op jit(solution)/shard_map/jit(_take)/gather | solution.py:108
  64.7 8.3 %fusion.2 = f32[180,96,128]{2,1,0:T(8,128)S(1)} fusion(bf16[20,128,128]{2,1,0:T(8,128)(2,1)} %collective-permute-done.3, bf16[160,128,128]{2,1,0:T(8,128)(2,1)} %param.14, bf16[180,96,128]{2,1,0:T(8,128)(2,1)} %gather_fusion, pred[180]{0:T(512)(128)(4,1)S(1)} %compare_and_fusion), kind=kOutput, calls=%fused_computation.4 | convolution fusion | flops 571392000 | bytes 19169460 | tf_op jit(solution)/shard_map/ctb,tab->tca/dot_general | solution.py:109
  73.0 0.0 copy-start.2
  73.0 0.0 copy-start.3
  73.1 8.7 %fusion = f32[96,128,32]{1,2,0:T(8,128)S(1)} fusion(f32[180,96,128]{2,1,0:T(8,128)S(1)} %fusion.2, s32[180]{0:T(256)S(1)} %add_subtract_fusion.2), kind=kOutput, calls=%fused_computation.2 | convolution fusion | flops 849352320 | bytes 10420944 | tf_op jit(solution)/shard_map/tw,tca->cwa/dot_general | solution.py:112
  81.8 2.5 %fusion.17 = f32[96,4096]{1,0:T(8,128)} fusion(f32[96,4096]{1,0:T(8,128)S(1)} %copy-done.2, f32[12,8,32,128]{3,2,1,0:T(8,128)S(1)} %bitcast.46, f32[16,4096]{1,0:T(8,128)S(1)} %fusion.30, f32[64,4096]{1,0:T(8,128)S(1)} %copy-done.3, f32[16,4096]{1,0:T(8,128)S(1)} %copy-done.4, f32[4096]{0:T(1024)S(1)} %reshape.150), kind=kLoop, calls=%fused_computation.25 | loop fusion | flops 2359296 | bytes 6307840 | tf_op jit(solution)/shard_map/add | solution.py:128
  (32 shorter events, 0.1 us)
Async XLA Ops:
  0.6 16.8 %copy-start = (f32[64,64]{1,0:T(8,128)S(1)}, f32[64,64]{1,0:T(8,128)}, u32[]{:S(2)}) copy-start(f32[64,64]{1,0:T(8,128)} %param.20) | copy-start | bytes 49156
  0.6 16.8 %copy-start.1 = (f32[96,4096]{1,0:T(8,128)S(1)}, f32[96,4096]{1,0:T(8,128)}, u32[]{:S(2)}) copy-start(f32[96,4096]{1,0:T(8,128)} %param.11) | copy-start | bytes 4718596
  0.7 10.8 %copy-start.5 = (s32[160]{0:T(256)S(1)}, s32[160]{0:T(256)}, u32[]{:S(2)}) copy-start(s32[160]{0:T(256)} %param.13) | copy-start | bytes 1924
  0.7 15.4 %copy-start.6 = (s32[160]{0:T(256)S(1)}, s32[160]{0:T(256)}, u32[]{:S(2)}) copy-start(s32[160]{0:T(256)} %param.12) | copy-start | bytes 1924
  0.7 16.8 %copy-start.10 = (f32[64]{0:T(128)S(1)}, f32[64]{0:T(128)}, u32[]{:S(2)}) copy-start(f32[64]{0:T(128)} %param.21) | copy-start | bytes 772
  2.3 57.3 %collective-permute-start.1 = (bf16[96,4096]{1,0:T(8,128)(2,1)S(1)}, bf16[96,4096]{1,0:T(8,128)(2,1)}, u32[]{:S(2)}, u32[]{:S(2)}) collective-permute-start(bf16[96,4096]{1,0:T(8,128)(2,1)S(1)} %convert_element_type.29), channel_id=1, source_target_pairs={{0,1},{1,2},{2,3},{3,4},{4,5},{5,6},{6,7},{7,8},{8,9},{9,10},{10,1... | collective-permute-start | bytes 2359304 | tf_op jit(solution)/shard_map/ppermute | solution.py:27
  5.7 53.9 %collective-permute-start.2 = (bf16[96,4096]{1,0:T(8,128)(2,1)S(1)}, bf16[96,4096]{1,0:T(8,128)(2,1)}, u32[]{:S(2)}, u32[]{:S(2)}) collective-permute-start(bf16[96,4096]{1,0:T(8,128)(2,1)S(1)} %convert_element_type.29), channel_id=1, source_target_pairs={{1,0},{2,1},{3,2},{4,3},{5,4},{6,5},{7,6},{8,7},{9,8},{10,9},{11,1... | collective-permute-start | bytes 2359304 | tf_op jit(solution)/shard_map/ppermute | solution.py:28
  11.5 34.3 %collective-permute-start = (s32[20]{0:T(128)S(1)}, s32[20]{0:T(128)S(1)}, u32[]{:S(2)}, u32[]{:S(2)}) collective-permute-start(s32[20]{0:T(128)S(1)} %slice.18), channel_id=1, source_target_pairs={{1,0},{2,1},{3,2},{4,3},{5,4},{6,5},{7,6},{9,8},{10,9},{11,10},{12... | collective-permute-start | bytes 248 | tf_op jit(solution)/shard_map/ppermute | solution.py:36
  14.8 50.0 %collective-permute-start.3 = (bf16[20,128,128]{2,1,0:T(8,128)(2,1)}, bf16[20,128,128]{2,1,0:T(8,128)(2,1)}, u32[]{:S(2)}, u32[]{:S(2)}) collective-permute-start(bf16[20,128,128]{2,1,0:T(8,128)(2,1)} %slice.19), channel_id=1, source_target_pairs={{1,0},{2,1},{3,2},{4,3},{5,4},{6,5},{7,6},{9,8},{10,9},{11,10},{12... | collective-permute-start | bytes 1966088 | tf_op jit(solution)/shard_map/ppermute | solution.py:36
  16.1 41.6 %collective-permute-start.4 = (s32[20]{0:T(128)S(1)}, s32[20]{0:T(128)S(1)}, u32[]{:S(2)}, u32[]{:S(2)}) collective-permute-start(s32[20]{0:T(128)S(1)} %slice.20), channel_id=1, source_target_pairs={{1,0},{2,1},{3,2},{4,3},{5,4},{6,5},{7,6},{9,8},{10,9},{11,10},{12... | collective-permute-start | bytes 248 | tf_op jit(solution)/shard_map/ppermute | solution.py:36
  17.5 2.8 %copy-start.8 = (s32[128]{0:T(128)S(1)}, s32[128]{0:T(128)}, u32[]{:S(2)}) copy-start(s32[128]{0:T(128)} %param.15) | copy-start | bytes 1540
  17.5 3.2 %copy-start.7 = (f32[64,16]{0,1:T(8,128)S(1)}, f32[64,16]{0,1:T(8,128)}, u32[]{:S(2)}) copy-start(f32[64,16]{0,1:T(8,128)} %param.19) | copy-start | bytes 12292
  17.5 3.2 %copy-start.11 = (f32[16]{0:T(128)S(1)}, f32[16]{0:T(128)}, u32[]{:S(2)}) copy-start(f32[16]{0:T(128)} %param.17) | copy-start | bytes 196
  17.5 3.2 %copy-start.12 = (f32[64]{0:T(128)S(1)}, f32[64]{0:T(128)}, u32[]{:S(2)}) copy-start(f32[64]{0:T(128)} %param.18) | copy-start | bytes 772
  20.1 3.0 %copy-start.9 = (s32[128]{0:T(128)S(1)}, s32[128]{0:T(128)}, u32[]{:S(2)}) copy-start(s32[128]{0:T(128)} %param.16) | copy-start | bytes 1540
  27.6 30.2 %all-to-all-start = ((f32[8,16,1]{1,2,0:T(1,128)}), f32[8,16,1]{1,2,0:T(1,128)S(1)}, u32[]{:S(2)}, u32[]{:S(2)}) async-start(f32[8,16,1]{1,2,0:T(1,128)} %bitcast.9), calls=%async_computation | async-start | bytes 8192 | tf_op jit(solution)/shard_map/all_to_all | solution.py:125
  73.0 8.7 %copy-start.2 = (f32[96,4096]{1,0:T(8,128)S(1)}, f32[96,4096]{1,0:T(8,128)}, u32[]{:S(2)}) copy-start(f32[96,4096]{1,0:T(8,128)} %param.11) | copy-start | bytes 4718596
  73.0 8.7 %copy-start.3 = (f32[64,4096]{1,0:T(8,128)S(1)}, f32[64,4096]{1,0:T(8,128)}, u32[]{:S(2)}) copy-start(f32[64,4096]{1,0:T(8,128)} %fusion.10) | copy-start | bytes 3145732
  73.0 8.7 %copy-start.4 = (f32[16,4096]{1,0:T(8,128)S(1)}, f32[16,4096]{1,0:T(8,128)}, u32[]{:S(2)}) copy-start(f32[16,4096]{1,0:T(8,128)} %fusion.12) | copy-start | bytes 786436
where the time goes:
time: 84.7 us; the launch traced here: 84.3 us
  matrix products  28.1 us (33%)
  starting transfers between devices  21.1 us (25%)
  other arithmetic  12 us (14%)
  waiting for transfers between devices  11.8 us (14%)
  local copies, waits for them, and re-layouts  10.3 us (12%)
  between operations  0.99 us (1%)
    ppermute x3, waiting for transfers between devices, from_behind(): lax.ppermute(value, axis, [(source, source + steps) for source in range(i...  11.8 us
    dot_general x1, matrix products, per_device(): jnp.einsum('tw,tca->cwa', onehot, contrib, precision=highest)  8.67 us
    dot_general x1, matrix products, per_device(): jnp.einsum('ctb,tab->tca', picked, all_data, preferred_element_type=jnp.f...  8.27 us
    all_to_all x1, starting transfers between devices, per_device(): lax.all_to_all(local_sums[send_order], 'dev', split_axis=0, concat_axis=0...  8.09 us
    ppermute x1, starting transfers between devices, with_halo(): after = lax.ppermute(initial, axis, down)  5.73 us
    dot_general x1, matrix products, ecosystem(): jnp.dot(graze_preference.T, graze_rate, precision=highest)  4.51 us
    ppermute x3, starting transfers between devices, from_behind(): lax.ppermute(value, axis, [(source, source + steps) for source in range(i...  3.86 us
    ppermute x1, starting transfers between devices, with_halo(): before = lax.ppermute(last, axis, up)  3.43 us
  transfers between devices with their start and end apart: 6, of which 1 were waited for; matrix products, arithmetic and copies ran while one was open for 33% of the time, Pallas kernels for 0%

commit v1 on v0

v1 whole, which is shorter than its diff:
```python
import jax
import jax.numpy as jnp
from jax import lax
from jax.experimental import pallas as pl
from jax.experimental.pallas import tpu as pltpu
from jax.sharding import PartitionSpec as P

NUT = 16
PLK = 64
LEV = 32
REACH = 16
LANES = 128
CHUNK = 256

HIGHEST = lax.Precision.HIGHEST
WATER_DECAY = 0.03
SHADE_DECAY = 0.05
EFFICIENCY = 0.3
MORTALITY = 0.1
REMINERAL = 0.2
TIMESTEP = 0.5
F32 = jnp.float32
BF16 = jnp.bfloat16
CHAIN = ("grp", "dev")


def chain_shift(x, step):
    count = lax.axis_size(CHAIN)
    pairs = [(i, i + step) for i in range(count) if 0 <= i + step < count]
    return lax.ppermute(x, CHAIN, pairs)


def group_shift(x, step):
    count = lax.axis_size("dev")
    pairs = [(i, i + step) for i in range(count) if 0 <= i + step < count]
    return lax.ppermute(x, "dev", pairs)


def iota(shape, dim):
    return lax.broadcasted_iota(jnp.int32, shape, dim)


def rows_dot(a, b, precision=None):
    return lax.dot_general(
        a, b, (((1,), (1,)), ((), ())), precision=precision, preferred_element_type=F32
    )


def dot(a, b, precision=None):
    return jnp.dot(a, b, precision=precision, preferred_element_type=F32)


def round_kernel(x_ref, out_ref):
    out_ref[...] = x_ref[...].astype(BF16)


def rounded(x, start, width, parts=2):
    rows, piece = x.shape[0], width // parts
    return pl.pallas_call(
        round_kernel,
        out_shape=jax.ShapeDtypeStruct((rows, width), BF16),
        grid=(parts,),
        in_specs=[pl.BlockSpec((rows, piece), lambda i: (0, start // piece + i))],
        out_specs=pl.BlockSpec((rows, piece), lambda i: (0, i)),
        compiler_params=pltpu.CompilerParams(vmem_limit_bytes=4 << 20),
        cost_estimate=pl.CostEstimate(
            flops=rows * width, bytes_accessed=rows * width * 6, transcendentals=0
        ),
    )(x)


def ecosystem_kernel(
    x_ref, tiles_ref, rows_ref, cols_ref, level_ref, owner_ref, half_ref, rate_ref,
    uptake_ref, prefer_ref, graze_ref, after_low_ref, after_high_ref,
    base_ref, send_ref, more_ref, index_ref, light_ref, wet_ref, sums_ref, sem,
):
    spill = pltpu.make_async_copy(tiles_ref.at[pl.ds(0, more_ref.shape[0])], more_ref, sem)
    spill.start()
    index_ref[0:1, :] = rows_ref[:, :LANES]
    index_ref[1:2, :] = cols_ref[:, :LANES]
    blocks = x_ref.shape[1] // LANES
    per_block = LANES // LEV
    columns = level_ref.shape[1]
    devices = send_ref.shape[0]

    mine = iota((blocks, columns), 1) // per_block == iota((blocks, columns), 0)
    spread = (
        iota((columns, LANES), 0) % per_block == iota((columns, LANES), 1) // LEV
    ).astype(F32)
    levels = level_ref[...].astype(F32)
    counts = dot(jnp.where(mine, levels, 0.0), spread, HIGHEST)
    depth = (iota((blocks, LANES), 1) % LEV).astype(F32)
    wet = (depth < counts).astype(F32)
    wet_ref[...] = wet

    for i in range(blocks):
        plankton = x_ref[NUT : NUT + PLK, i * LANES : (i + 1) * LANES]
        sums_ref[i : i + 1, :] = jnp.sum(plankton, axis=0, keepdims=True)
    upper, lower = iota((LANES, LANES), 0), iota((LANES, LANES), 1)
    above = ((upper // LEV == lower // LEV) & (upper < lower)).astype(F32)
    shading = dot(sums_ref[...] / PLK * wet, above, HIGHEST)
    light_ref[...] = jnp.exp(-WATER_DECAY * depth - SHADE_DECAY * shading)

    def upright(ref):
        n = ref.shape[1]
        return jnp.sum(
            jnp.where(iota((n, n), 0) == iota((n, n), 1), ref[...], 0.0), axis=1, keepdims=True
        )

    half = upright(half_ref)
    rate = upright(rate_ref)
    most = upright(graze_ref)
    prefer = prefer_ref[...]
    uptake = uptake_ref[...].T
    prefer_b = prefer.astype(BF16)
    prefer_t = prefer.T.astype(BF16)
    uptake_b = uptake.astype(BF16)
    uptake_t = uptake_ref[...].astype(BF16)
    quarter = (iota((NUT, PLK), 1) // (PLK // NUT) == iota((NUT, PLK), 0)).astype(BF16)
    span = CHUNK // LANES

    def row_of(ref, k):
        return jnp.concatenate([ref[pl.ds(k * span + s, 1), :] for s in range(span)], axis=1)

    def step(k, carry):
        at = pl.ds(pl.multiple_of(k * CHUNK, CHUNK), CHUNK)
        nutrient = x_ref[:NUT, at]
        plankton = x_ref[NUT : NUT + PLK, at]
        detritus = x_ref[NUT + PLK :, at]
        sun = row_of(light_ref, k)
        mask = row_of(wet_ref, k)
        monod = nutrient / (nutrient + half)
        limitation = dot(uptake_b, monod.astype(BF16))
        capacity = rate * sun * plankton
        growth = capacity * limitation
        food = dot(prefer_b, plankton.astype(BF16))
        graze = most * plankton / (1.0 + food)
        grazed = plankton * dot(prefer_t, graze.astype(BF16))
        eaten = graze * food
        d_plankton = growth - grazed + EFFICIENCY * eaten - MORTALITY * plankton
        d_nutrient = -monod * dot(uptake_t, capacity.astype(BF16)) + REMINERAL * detritus
        waste = (1.0 - EFFICIENCY) * eaten + MORTALITY * plankton
        waste_high = waste.astype(BF16)
        waste_low = (waste - waste_high.astype(F32)).astype(BF16)
        d_detritus = dot(quarter, waste_high) + dot(quarter, waste_low) - REMINERAL * detritus
        scale = TIMESTEP * mask
        base_ref[:NUT, at] = nutrient + scale * d_nutrient
        base_ref[NUT : NUT + PLK, at] = plankton + scale * d_plankton
        base_ref[NUT + PLK :, at] = detritus + scale * d_detritus
        total = jnp.sum(growth, axis=0, keepdims=True) / PLK * mask
        for s in range(span):
            sums_ref[pl.ds(k * span + s, 1), :] = total[:, s * LANES : (s + 1) * LANES]
        return carry

    lax.fori_loop(0, x_ref.shape[1] // CHUNK, step, 0)

    by_column = dot(sums_ref[...], spread.T, HIGHEST)
    production = jnp.sum(jnp.where(mine, by_column, 0.0), axis=0, keepdims=True)
    owned = owner_ref[...] == iota((devices, columns), 0)
    before = (iota((columns, columns), 0) < iota((columns, columns), 1)).astype(BF16)
    earlier = dot(owned.astype(BF16), before)
    rank = jnp.sum(jnp.where(owned, earlier, 0.0), axis=0, keepdims=True).astype(jnp.int32)
    place = (rank == iota((LANES, columns), 0)).astype(F32)
    send_ref[...] = rows_dot(jnp.where(owned, production, 0.0), place, HIGHEST)
    spill.wait()


def tiles_kernel(index_ref, tiles_ref, low_ref, high_ref, left_ref, right_ref,
                 base_ref, out_ref, near_ref, held_ref, sems):
    blocks = base_ref.shape[1] // LANES
    half = blocks // 2
    width = half * LANES
    pieces = sems.shape[0]
    batch = held_ref.shape[0] // pieces
    first = (lax.axis_index("grp") * lax.axis_size("dev") + lax.axis_index("dev")) * blocks

    def load(k):
        at = pl.ds(k * batch, batch)
        return pltpu.make_async_copy(tiles_ref.at[at], held_ref.at[at], sems.at[k])

    for k in range(pieces):
        load(k).start()
    out_ref[...] = base_ref[...]
    for k, ref in enumerate((left_ref, low_ref, high_ref, right_ref)):
        near_ref[:, k * width : (k + 1) * width] = ref[...]

    def piece(k, carry):
        load(k).wait()
        for j in range(batch):
            t = k * batch + j
            slot = index_ref[0, t] - first
            mine = (slot >= 0) & (slot < blocks)
            slot = jnp.clip(slot, 0, blocks - 1)
            col = jnp.clip(index_ref[1, t] - first + half, 0, 4 * half - 1)
            cells = near_ref[:, pl.ds(pl.multiple_of(col * LANES, LANES), LANES)]
            part = rows_dot(cells, held_ref[t])
            at = pl.ds(pl.multiple_of(slot * LANES, LANES), LANES)
            out_ref[:, at] += jnp.where(mine, part, 0.0)
        return carry

    lax.fori_loop(0, pieces, piece, 0)


def call_tiles(index, tiles, low, high, left, right, base, batch, space):
    count, size = tiles.shape[0], tiles.shape[1]
    channels, cells = base.shape
    whole = lambda a: pl.BlockSpec(a.shape, lambda i, *_: (0, 0))
    return pl.pallas_call(
        tiles_kernel,
        out_shape=jax.ShapeDtypeStruct(base.shape, F32),
        grid_spec=pltpu.PrefetchScalarGridSpec(
            num_scalar_prefetch=1,
            grid=(1,),
            in_specs=[pl.BlockSpec(memory_space=space)]
            + [whole(a) for a in (low, high, left, right, base)],
            out_specs=whole(base),
            scratch_shapes=[
                pltpu.VMEM((channels, 2 * cells), BF16),
                pltpu.VMEM((count, size, size), BF16),
                pltpu.SemaphoreType.DMA((count // batch,)),
            ],
        ),
        compiler_params=pltpu.CompilerParams(vmem_limit_bytes=24 << 20),
        cost_estimate=pl.CostEstimate(
            flops=2 * count * channels * size * size,
            bytes_accessed=tiles.size * 2 + base.size * 12,
            transcendentals=0,
        ),
    )(index, tiles, low, high, left, right, base)


def per_device(
    tracer, tile_rows, tile_cols, tile_values, level_counts, column_owner,
    half_saturation, growth_rate, uptake, graze_preference, graze_maximum,
):
    channels, cells = tracer.shape
    tile_total, block = tile_values.shape[0], tile_values.shape[1]
    spill = tile_total // 8
    half = cells // 2
    assert half >= REACH * block and block == LANES
    devices = lax.axis_size("dev")

    high = rounded(tracer, half, half)
    low = rounded(tracer, 0, half)
    left = chain_shift(high, 1)
    right = chain_shift(low, -1)

    whole = lambda *shape: pl.BlockSpec(shape, lambda i: (0,) * len(shape))
    base, send, spilled, spilled_index = pl.pallas_call(
        ecosystem_kernel,
        out_shape=(
            jax.ShapeDtypeStruct((channels, cells), F32),
            jax.ShapeDtypeStruct((devices, LANES), F32),
            jax.ShapeDtypeStruct((spill, block, block), BF16),
            jax.ShapeDtypeStruct((2, LANES), jnp.int32),
        ),
        grid=(1,),
        in_specs=[
            whole(channels, cells),
            pl.BlockSpec(memory_space=pltpu.HBM),
            whole(1, tile_total),
            whole(1, tile_total),
            whole(1, level_counts.shape[0]),
            whole(1, column_owner.shape[0]),
            whole(1, NUT),
            whole(1, PLK),
            whole(NUT, PLK),
            whole(PLK, PLK),
            whole(1, PLK),
            pl.BlockSpec(memory_space=pl.ANY),
            pl.BlockSpec(memory_space=pl.ANY),
        ],
        out_specs=(
            whole(channels, cells),
            whole(devices, LANES),
            whole(spill, block, block),
            whole(2, LANES),
        ),
        scratch_shapes=[pltpu.VMEM((cells // LANES, LANES), F32)] * 3 + [pltpu.SemaphoreType.DMA],
        compiler_params=pltpu.CompilerParams(vmem_limit_bytes=20 << 20),
        cost_estimate=pl.CostEstimate(
            flops=cells * 30000, bytes_accessed=channels * cells * 8, transcendentals=cells
        ),
    )(
        tracer,
        tile_values,
        tile_rows[None, :],
        tile_cols[None, :],
        level_counts[None, :],
        column_owner[None, :],
        half_saturation[None, :],
        growth_rate[None, :],
        uptake.T,
        graze_preference,
        graze_maximum[None, :],
        low,
        high,
    )
    share = level_counts.shape[0] // devices
    received = lax.all_to_all(send[:, :share], "dev", split_axis=0, concat_axis=0)
    production = received.reshape(-1)
    more_index = group_shift(spilled_index, -1)
    more_tiles = group_shift(spilled, -1)

    index = jnp.stack([tile_rows, tile_cols])
    mid = call_tiles(index, tile_values, low, high, left, right, base, 16, pltpu.HBM)
    updated = call_tiles(
        more_index, more_tiles, low, high, left, right, mid, spill, pl.ANY
    )
    return updated, production


def solution(mesh):
    return jax.shard_map(
        per_device,
        mesh=mesh,
        in_specs=(
            P(None, CHAIN),
            P(CHAIN),
            P(CHAIN),
            P(CHAIN, None, None),
            P(CHAIN),
            P(CHAIN),
            P(),
            P(),
            P(),
            P(),
            P(),
        ),
        out_specs=(P(None, CHAIN), P(CHAIN)),
        check_vma=False,
    )
```

time: 84.7 us -> 64.3 us (0.76)
  the two profiles are of different devices: /device:TPU:2 before, /device:TPU:0 now
where the time goes in v1:
time: 64.3 us; the launch traced here: 63.9 us
  waiting for transfers between devices  19.2 us (30%)
  starting transfers between devices  17.7 us (28%)
  Pallas kernels  17 us (26%)
  local copies, waits for them, and re-layouts  8.44 us (13%)
  between operations  0.85 us (1%)
  other arithmetic  0.67 us (1%)
    all_to_all x1, waiting for transfers between devices, per_device(): lax.all_to_all(send[:, :share], 'dev', split_axis=0, concat_axis=0)  19.2 us
    pallas_call x2, Pallas kernels, call_tiles(): pl.pallas_call(tiles_kernel, out_shape=jax.ShapeDtypeStruct(base.shape, F...  9.7 us
    all_to_all x1, starting transfers between devices, per_device(): lax.all_to_all(send[:, :share], 'dev', split_axis=0, concat_axis=0)  8.29 us
    unnamed x26, local copies, waits for them, and re-layouts  7.34 us
    pallas_call x1, Pallas kernels, per_device(): pl.pallas_call(ecosystem_kernel, out_shape=(jax.ShapeDtypeStruct((channel...  6.95 us
    ppermute x2, starting transfers between devices, chain_shift(): return lax.ppermute(x, CHAIN, pairs)  6.84 us
    ppermute x2, starting transfers between devices, group_shift(): return lax.ppermute(x, 'dev', pairs)  2.57 us
  transfers between devices with their start and end apart: 5, of which 1 were waited for; matrix products, arithmetic and copies ran while one was open for 3% of the time, Pallas kernels for 10%

profile of v1, /device:TPU:0, one launch (start us, length us, event | category | flops | bytes accessed | tf_op | source)
XLA Modules:
  0.0 63.9 jit_solution(1179384402218126150)
XLA Ops:
  0.6 0.0 copy-start.2
  0.6 1.4 %copy-done.2 = f32[96,4096]{1,0:T(8,128)S(1)} copy-done((f32[96,4096]{1,0:T(8,128)S(1)}, f32[96,4096]{1,0:T(8,128)}, u32[]{:S(2)}) %copy-start.2) | copy-done | bytes 1572888
  2.0 0.0 copy-start.3
  2.0 0.0 copy-start.4
  2.0 0.0 copy-start.5
  2.0 0.0 copy-start.6
  2.1 0.0 copy-start.7
  2.1 0.0 copy-start.8
  2.1 0.0 copy-start.9
  2.1 0.0 copy-start.10
  2.1 0.0 copy-start.11
  2.1 0.0 copy-start.12
  2.1 0.2 shard_map.122.after_low_ref.low_ref
  2.3 0.2 shard_map.123.after_high_ref.high_ref
  2.5 0.9 %copy-done.3 = f32[96,4096]{1,0:T(8,128)S(1)} copy-done((f32[96,4096]{1,0:T(8,128)S(1)}, f32[96,4096]{1,0:T(8,128)}, u32[]{:S(2)}) %copy-start.3) | copy-done | bytes 1572888
  3.5 0.0 copy-done.4
  3.5 0.0 copy-done.5
  3.5 0.0 copy-done.6
  3.5 0.0 copy-done.7
  3.5 0.0 copy-done.8
  3.5 0.0 copy-done.9
  3.5 0.0 copy-done.10
  3.5 0.0 copy-done.11
  3.5 0.0 copy-done.12
  3.5 0.0 copy-start
  3.5 2.5 %copy-done = bf16[160,128,128]{2,1,0:T(8,128)(2,1)S(1)} copy-done((bf16[160,128,128]{2,1,0:T(8,128)(2,1)S(1)}, bf16[160,128,128]{2,1,0:T(8,128)(2,1)}, u32[]{:S(2)}) %copy-start) | copy-done | bytes 5242904
  6.0 6.9 %shard_map.124 = (f32[96,4096]{1,0:T(8,128)S(1)}, f32[8,128]{1,0:T(8,128)}, bf16[20,128,128]{2,1,0:T(8,128)(2,1)}, s32[2,128]{1,0:T(2,128)S(1)}) custom-call(f32[96,4096]{1,0:T(8,128)S(1)} %copy-done.3, bf16[160,128,128]{2,1,0:T(8,128)(2,1)S(1)} %copy-done, s32[1,160]{1,0:T(1,128)S(1)} %bitcast.13, s32[1,160]{1,0:T(1,128)S(1)} %bitcast.15, ...), custom_call_target="tpu_custom_call" | custom-call | flops 122880000 | bytes 3145728 | tf_op jit(solution)/shard_map/pallas_call | solution.py:249
  13.0 1.3 %collective-permute-start.1 = (bf16[20,128,128]{2,1,0:T(8,128)(2,1)}, bf16[20,128,128]{2,1,0:T(8,128)(2,1)}, u32[]{:S(2)}, u32[]{:S(2)}) collective-permute-start(bf16[20,128,128]{2,1,0:T(8,128)(2,1)} %get-tuple-element.7), channel_id=1, source_target_pairs={{1,0},{2,1},{3,2},{4,3},{5,4},{6,5},{7,6},{9,8},{10,9},{11,10},{12... | collective-permute-start | bytes 1966088 | tf_op jit(solution)/shard_map/ppermute | solution.py:36
  14.3 5.6 %collective-permute-start.2 = (bf16[96,2048]{1,0:T(8,128)(2,1)S(1)}, bf16[96,2048]{1,0:T(8,128)(2,1)S(1)}, u32[]{:S(2)}, u32[]{:S(2)}) collective-permute-start(bf16[96,2048]{1,0:T(8,128)(2,1)S(1)} %shard_map.123.after_high_ref.high_ref), channel_id=1, source_target_pairs={{0,1},{1,2},{2,3},{3,4},{4,5},{5,6},{6,7},{7,8},{8,9},{9,10},{10,1... | collective-permute-start | bytes 1179656 | tf_op jit(solution)/shard_map/ppermute | solution.py:30
  19.8 1.3 %collective-permute-start.3 = (bf16[96,2048]{1,0:T(8,128)(2,1)S(1)}, bf16[96,2048]{1,0:T(8,128)(2,1)S(1)}, u32[]{:S(2)}, u32[]{:S(2)}) collective-permute-start(bf16[96,2048]{1,0:T(8,128)(2,1)S(1)} %shard_map.122.after_low_ref.low_ref), channel_id=1, source_target_pairs={{1,0},{2,1},{3,2},{4,3},{5,4},{6,5},{7,6},{8,7},{9,8},{10,9},{11,1... | collective-permute-start | bytes 1179656 | tf_op jit(solution)/shard_map/ppermute | solution.py:30
  21.1 8.3 %all-to-all-start = ((f32[8,1,16]{2,1,0:T(1,128)}), f32[8,1,16]{2,1,0:T(1,128)S(1)}, u32[]{:S(2)}, u32[]{:S(2)}) async-start(f32[8,1,16]{2,1,0:T(1,128)} %bitcast.9), calls=%async_computation | async-start | bytes 8192 | tf_op jit(solution)/shard_map/all_to_all | solution.py:300
  29.4 1.3 %collective-permute-start = (s32[2,128]{1,0:T(2,128)S(1)}, s32[2,128]{1,0:T(2,128)S(1)}, u32[]{:S(2)}, u32[]{:S(2)}) collective-permute-start(s32[2,128]{1,0:T(2,128)S(1)} %get-tuple-element.6), channel_id=1, source_target_pairs={{1,0},{2,1},{3,2},{4,3},{5,4},{6,5},{7,6},{9,8},{10,9},{11,10},{12... | collective-permute-start | bytes 3080 | tf_op jit(solution)/shard_map/ppermute | solution.py:36
  30.7 19.2 %all-to-all-done = f32[8,1,16]{2,1,0:T(1,128)S(1)} async-done(((f32[8,1,16]{2,1,0:T(1,128)}), f32[8,1,16]{2,1,0:T(1,128)S(1)}, u32[]{:S(2)}, u32[]{:S(2)}) %all-to-all-start) | async-done | bytes 544 | tf_op jit(solution)/shard_map/all_to_all | solution.py:300
  49.9 0.5 broadcast.3
  50.4 0.7 %reduce.3 = f32[8,16]{1,0:T(8,128)S(1)} reduce(f32[8,1,16]{2,1,0:T(1,128)S(1)} %all-to-all-done, f32[]{:T(128)} %broadcast.3), dimensions={1}, to_apply=%all_to_all.7.reduce_sub_computation.3 | reduce | bytes 1028 | tf_op jit(solution)/shard_map/all_to_all | solution.py:300
  51.1 0.6 reshape.10
  51.7 0.0 collective-permute-done.2.left_ref
  51.7 0.0 collective-permute-done.3.right_ref
  51.7 0.0 copy-start.1
  51.7 2.5 %copy-done.1 = bf16[160,128,128]{2,1,0:T(8,128)(2,1)S(1)} copy-done((bf16[160,128,128]{2,1,0:T(8,128)(2,1)S(1)}, bf16[160,128,128]{2,1,0:T(8,128)(2,1)}, u32[]{:S(2)}) %copy-start.1) | copy-done | bytes 5242904
  54.2 6.3 %shard_map.125.base_ref = f32[96,4096]{1,0:T(8,128)S(1)} custom-call(s32[2,160]{1,0:T(2,128)S(1)} %pad_add_fusion.index_ref, bf16[160,128,128]{2,1,0:T(8,128)(2,1)S(1)} %copy-done.1, bf16[96,2048]{1,0:T(8,128)(2,1)S(1)} %shard_map.122.after_low_ref.low_ref, bf16[96,2048]{1,0:T(8,128)(2,1)S(1)} %shard_map.123.after_high_ref.high_ref, ...), custom_call_target="tpu_custom_call" | custom-call | flops 503316480 | bytes 9961472 | tf_op jit(solution)/shard_map/pallas_call | solution.py:208
  60.5 0.0 collective-permute-done.index_ref
  60.5 0.0 collective-permute-done.1.tiles_ref
  60.5 3.4 %shard_map.126 = f32[96,4096]{1,0:T(8,128)} custom-call(s32[2,128]{1,0:T(2,128)S(1)} %collective-permute-done.index_ref, bf16[20,128,128]{2,1,0:T(8,128)(2,1)} %collective-permute-done.1.tiles_ref, bf16[96,2048]{1,0:T(8,128)(2,1)S(1)} %shard_map.122.after_low_ref.low_ref, bf16[96,2048]{1,0:T(8,128)(2,1)S(1)} %shard_map.123.after_high_ref.high_ref, ...), custom_call_target="tpu_custom_call" | custom-call | flops 62914560 | bytes 5373952 | tf_op jit(solution)/shard_map/pallas_call | solution.py:208
  (1 shorter events, 0.0 us)
Async XLA Ops:
  0.6 1.4 %copy-start.2 = (f32[96,4096]{1,0:T(8,128)S(1)}, f32[96,4096]{1,0:T(8,128)}, u32[]{:S(2)}) copy-start(f32[96,4096]{1,0:T(8,128)} %x_ref.5) | copy-start | bytes 4718596
  2.0 1.4 %copy-start.3 = (f32[96,4096]{1,0:T(8,128)S(1)}, f32[96,4096]{1,0:T(8,128)}, u32[]{:S(2)}) copy-start(f32[96,4096]{1,0:T(8,128)} %x_ref.5) | copy-start | bytes 4718596
  2.0 1.4 %copy-start.4 = (f32[64,64]{1,0:T(8,128)S(1)}, f32[64,64]{1,0:T(8,128)}, u32[]{:S(2)}) copy-start(f32[64,64]{1,0:T(8,128)} %prefer_ref.1) | copy-start | bytes 49156
  2.0 1.4 %copy-start.5 = (f32[64,16]{0,1:T(8,128)S(1)}, f32[64,16]{0,1:T(8,128)}, u32[]{:S(2)}) copy-start(f32[64,16]{0,1:T(8,128)} %param.19) | copy-start | bytes 12292
  2.0 1.4 %copy-start.6 = (s32[160]{0:T(256)S(1)}, s32[160]{0:T(256)}, u32[]{:S(2)}) copy-start(s32[160]{0:T(256)} %param.12) | copy-start | bytes 1924
  2.1 1.4 %copy-start.7 = (s32[160]{0:T(256)S(1)}, s32[160]{0:T(256)}, u32[]{:S(2)}) copy-start(s32[160]{0:T(256)} %param.13) | copy-start | bytes 1924
  2.1 1.4 %copy-start.8 = (s32[128]{0:T(128)S(1)}, s32[128]{0:T(128)}, u32[]{:S(2)}) copy-start(s32[128]{0:T(128)} %param.15) | copy-start | bytes 1540
  2.1 1.4 %copy-start.9 = (s32[128]{0:T(128)S(1)}, s32[128]{0:T(128)}, u32[]{:S(2)}) copy-start(s32[128]{0:T(128)} %param.16) | copy-start | bytes 1540
  2.1 1.4 %copy-start.10 = (f32[16]{0:T(128)S(1)}, f32[16]{0:T(128)}, u32[]{:S(2)}) copy-start(f32[16]{0:T(128)} %param.17) | copy-start | bytes 196
  2.1 1.4 %copy-start.11 = (f32[64]{0:T(128)S(1)}, f32[64]{0:T(128)}, u32[]{:S(2)}) copy-start(f32[64]{0:T(128)} %param.18) | copy-start | bytes 772
  2.1 1.4 %copy-start.12 = (f32[64]{0:T(128)S(1)}, f32[64]{0:T(128)}, u32[]{:S(2)}) copy-start(f32[64]{0:T(128)} %param.21) | copy-start | bytes 772
  3.5 2.5 %copy-start = (bf16[160,128,128]{2,1,0:T(8,128)(2,1)S(1)}, bf16[160,128,128]{2,1,0:T(8,128)(2,1)}, u32[]{:S(2)}) copy-start(bf16[160,128,128]{2,1,0:T(8,128)(2,1)} %tiles_ref.3) | copy-start | bytes 15728644
  13.0 47.6 %collective-permute-start.1 = (bf16[20,128,128]{2,1,0:T(8,128)(2,1)}, bf16[20,128,128]{2,1,0:T(8,128)(2,1)}, u32[]{:S(2)}, u32[]{:S(2)}) collective-permute-start(bf16[20,128,128]{2,1,0:T(8,128)(2,1)} %get-tuple-element.7), channel_id=1, source_target_pairs={{1,0},{2,1},{3,2},{4,3},{5,4},{6,5},{7,6},{9,8},{10,9},{11,10},{12... | collective-permute-start | bytes 1966088 | tf_op jit(solution)/shard_map/ppermute | solution.py:36
  14.3 37.4 %collective-permute-start.2 = (bf16[96,2048]{1,0:T(8,128)(2,1)S(1)}, bf16[96,2048]{1,0:T(8,128)(2,1)S(1)}, u32[]{:S(2)}, u32[]{:S(2)}) collective-permute-start(bf16[96,2048]{1,0:T(8,128)(2,1)S(1)} %shard_map.123.after_high_ref.high_ref), channel_id=1, source_target_pairs={{0,1},{1,2},{2,3},{3,4},{4,5},{5,6},{6,7},{7,8},{8,9},{9,10},{10,1... | collective-permute-start | bytes 1179656 | tf_op jit(solution)/shard_map/ppermute | solution.py:30
  19.8 31.9 %collective-permute-start.3 = (bf16[96,2048]{1,0:T(8,128)(2,1)S(1)}, bf16[96,2048]{1,0:T(8,128)(2,1)S(1)}, u32[]{:S(2)}, u32[]{:S(2)}) collective-permute-start(bf16[96,2048]{1,0:T(8,128)(2,1)S(1)} %shard_map.122.after_low_ref.low_ref), channel_id=1, source_target_pairs={{1,0},{2,1},{3,2},{4,3},{5,4},{6,5},{7,6},{8,7},{9,8},{10,9},{11,1... | collective-permute-start | bytes 1179656 | tf_op jit(solution)/shard_map/ppermute | solution.py:30
  21.1 28.8 %all-to-all-start = ((f32[8,1,16]{2,1,0:T(1,128)}), f32[8,1,16]{2,1,0:T(1,128)S(1)}, u32[]{:S(2)}, u32[]{:S(2)}) async-start(f32[8,1,16]{2,1,0:T(1,128)} %bitcast.9), calls=%async_computation | async-start | bytes 8192 | tf_op jit(solution)/shard_map/all_to_all | solution.py:300
  29.4 31.1 %collective-permute-start = (s32[2,128]{1,0:T(2,128)S(1)}, s32[2,128]{1,0:T(2,128)S(1)}, u32[]{:S(2)}, u32[]{:S(2)}) collective-permute-start(s32[2,128]{1,0:T(2,128)S(1)} %get-tuple-element.6), channel_id=1, source_target_pairs={{1,0},{2,1},{3,2},{4,3},{5,4},{6,5},{7,6},{9,8},{10,9},{11,10},{12... | collective-permute-start | bytes 3080 | tf_op jit(solution)/shard_map/ppermute | solution.py:36
  51.7 2.5 %copy-start.1 = (bf16[160,128,128]{2,1,0:T(8,128)(2,1)S(1)}, bf16[160,128,128]{2,1,0:T(8,128)(2,1)}, u32[]{:S(2)}) copy-start(bf16[160,128,128]{2,1,0:T(8,128)(2,1)} %tiles_ref.3) | copy-start | bytes 15728644

commit v2 on v1

v2 whole, which is shorter than its diff:
```python
import functools

import jax
import jax.numpy as jnp
from jax import lax
from jax.experimental import pallas as pl
from jax.experimental.pallas import tpu as pltpu
from jax.sharding import PartitionSpec as P

NUT = 16
PLK = 64
LEV = 32
REACH = 16
LANES = 128
CHUNK = 256

HIGHEST = lax.Precision.HIGHEST
WATER_DECAY = 0.03
SHADE_DECAY = 0.05
EFFICIENCY = 0.3
MORTALITY = 0.1
REMINERAL = 0.2
TIMESTEP = 0.5
F32 = jnp.float32
BF16 = jnp.bfloat16
CHAIN = ("grp", "dev")


def chain_shift(x, step):
    count = lax.axis_size(CHAIN)
    pairs = [(i, i + step) for i in range(count) if 0 <= i + step < count]
    return lax.ppermute(x, CHAIN, pairs)


def group_shift(x, step):
    count = lax.axis_size("dev")
    pairs = [(i, i + step) for i in range(count) if 0 <= i + step < count]
    return lax.ppermute(x, "dev", pairs)


def iota(shape, dim):
    return lax.broadcasted_iota(jnp.int32, shape, dim)


def rows_dot(a, b, precision=None):
    return lax.dot_general(
        a, b, (((1,), (1,)), ((), ())), precision=precision, preferred_element_type=F32
    )


def dot(a, b, precision=None):
    return jnp.dot(a, b, precision=precision, preferred_element_type=F32)


def in_hbm(x):
    return pltpu.with_memory_space_constraint(x, pltpu.HBM)


VMEM_SPEC = pl.BlockSpec(memory_space=pltpu.VMEM)
HBM_SPEC = pl.BlockSpec(memory_space=pltpu.HBM)
ANY_SPEC = pl.BlockSpec(memory_space=pl.ANY)


def round_kernel(start, x_ref, out_ref, held_ref, sems):
    pieces = sems.shape[0]
    width = out_ref.shape[1] // pieces

    def load(k):
        return pltpu.make_async_copy(
            x_ref.at[:, pl.ds(start + k * width, width)],
            held_ref.at[:, pl.ds(k * width, width)],
            sems.at[k],
        )

    for k in range(pieces):
        load(k).start()
    for k in range(pieces):
        load(k).wait()
        at = slice(k * width, (k + 1) * width)
        out_ref[:, at] = held_ref[:, at].astype(BF16)


def rounded(x, start, width, pieces=4):
    rows = x.shape[0]
    return pl.pallas_call(
        functools.partial(round_kernel, start),
        out_shape=jax.ShapeDtypeStruct((rows, width), BF16),
        in_specs=[HBM_SPEC],
        out_specs=VMEM_SPEC,
        scratch_shapes=[pltpu.VMEM((rows, width), F32), pltpu.SemaphoreType.DMA((pieces,))],
        compiler_params=pltpu.CompilerParams(vmem_limit_bytes=4 << 20),
        cost_estimate=pl.CostEstimate(
            flops=rows * width, bytes_accessed=rows * width * 6, transcendentals=0
        ),
    )(x)


def pack_kernel(tiles_ref, rows_ref, cols_ref, after_low_ref, after_high_ref,
                more_ref, index_ref, sem):
    copy = pltpu.make_async_copy(tiles_ref.at[pl.ds(0, more_ref.shape[0])], more_ref, sem)
    copy.start()
    index_ref[0:1, :] = rows_ref[:, :LANES]
    index_ref[1:2, :] = cols_ref[:, :LANES]
    copy.wait()


def ecosystem_kernel(
    x_ref, level_ref, owner_ref, half_ref, rate_ref, uptake_ref, prefer_ref, graze_ref,
    after_ref, far_ref, send_ref, base_ref, light_ref, wet_ref, sums_ref, sem,
):
    blocks = x_ref.shape[1] // LANES
    per_block = LANES // LEV
    columns = level_ref.shape[1]
    devices, _, share = send_ref.shape

    mine = iota((blocks, columns), 1) // per_block == iota((blocks, columns), 0)
    spread = (
        iota((columns, LANES), 0) % per_block == iota((columns, LANES), 1) // LEV
    ).astype(F32)
    levels = level_ref[...].astype(F32)
    counts = dot(jnp.where(mine, levels, 0.0), spread, HIGHEST)
    depth = (iota((blocks, LANES), 1) % LEV).astype(F32)
    wet = (depth < counts).astype(F32)
    wet_ref[...] = wet

    for i in range(blocks):
        plankton = x_ref[NUT : NUT + PLK, i * LANES : (i + 1) * LANES]
        sums_ref[i : i + 1, :] = jnp.sum(plankton, axis=0, keepdims=True)
    upper, lower = iota((LANES, LANES), 0), iota((LANES, LANES), 1)
    above = ((upper // LEV == lower // LEV) & (upper < lower)).astype(F32)
    shading = dot(sums_ref[...] / PLK * wet, above, HIGHEST)
    light_ref[...] = jnp.exp(-WATER_DECAY * depth - SHADE_DECAY * shading)

    def upright(ref):
        n = ref.shape[1]
        return jnp.sum(
            jnp.where(iota((n, n), 0) == iota((n, n), 1), ref[...], 0.0), axis=1, keepdims=True
        )

    half = upright(half_ref)
    rate = upright(rate_ref)
    most = upright(graze_ref)
    prefer = prefer_ref[...]
    uptake = uptake_ref[...].T
    prefer_b = prefer.astype(BF16)
    prefer_t = prefer.T.astype(BF16)
    uptake_b = uptake.astype(BF16)
    uptake_t = uptake_ref[...].astype(BF16)
    quarter = (iota((NUT, PLK), 1) // (PLK // NUT) == iota((NUT, PLK), 0)).astype(BF16)
    span = CHUNK // LANES

    def row_of(ref, k):
        return jnp.concatenate([ref[pl.ds(k * span + s, 1), :] for s in range(span)], axis=1)

    def step(k, carry):
        at = pl.ds(pl.multiple_of(k * CHUNK, CHUNK), CHUNK)
        nutrient = x_ref[:NUT, at]
        plankton = x_ref[NUT : NUT + PLK, at]
        detritus = x_ref[NUT + PLK :, at]
        sun = row_of(light_ref, k)
        mask = row_of(wet_ref, k)
        monod = nutrient / (nutrient + half)
        limitation = dot(uptake_b, monod.astype(BF16))
        capacity = rate * sun * plankton
        growth = capacity * limitation
        food = dot(prefer_b, plankton.astype(BF16))
        graze = most * plankton / (1.0 + food)
        grazed = plankton * dot(prefer_t, graze.astype(BF16))
        eaten = graze * food
        d_plankton = growth - grazed + EFFICIENCY * eaten - MORTALITY * plankton
        d_nutrient = -monod * dot(uptake_t, capacity.astype(BF16)) + REMINERAL * detritus
        waste = (1.0 - EFFICIENCY) * eaten + MORTALITY * plankton
        waste_high = waste.astype(BF16)
        waste_low = (waste - waste_high.astype(F32)).astype(BF16)
        d_detritus = dot(quarter, waste_high) + dot(quarter, waste_low) - REMINERAL * detritus
        scale = TIMESTEP * mask
        base_ref[:NUT, at] = nutrient + scale * d_nutrient
        base_ref[NUT : NUT + PLK, at] = plankton + scale * d_plankton
        base_ref[NUT + PLK :, at] = detritus + scale * d_detritus
        total = jnp.sum(growth, axis=0, keepdims=True) / PLK * mask
        for s in range(span):
            sums_ref[pl.ds(k * span + s, 1), :] = total[:, s * LANES : (s + 1) * LANES]
        pltpu.make_async_copy(base_ref.at[:, at], far_ref.at[:, at], sem).start()
        return carry

    lax.fori_loop(0, x_ref.shape[1] // CHUNK, step, 0)

    by_column = dot(sums_ref[...], spread.T, HIGHEST)
    production = jnp.sum(jnp.where(mine, by_column, 0.0), axis=0, keepdims=True)
    owned = owner_ref[...] == iota((devices, columns), 0)
    before = (iota((columns, columns), 0) < iota((columns, columns), 1)).astype(BF16)
    earlier = dot(owned.astype(BF16), before)
    rank = jnp.sum(jnp.where(owned, earlier, 0.0), axis=0, keepdims=True).astype(jnp.int32)
    place = (rank == iota((LANES, columns), 0)).astype(F32)
    sorted_sums = rows_dot(jnp.where(owned, production, 0.0), place, HIGHEST)
    for o in range(devices):
        send_ref[o] = sorted_sums[o : o + 1, :share]
    pltpu.make_async_copy(base_ref, far_ref, sem).wait()


def place_of(index_ref, t, first, held):
    slot = index_ref[0, t] - first
    col = index_ref[1, t] - first
    col = jnp.clip(jnp.where(col < 0, col + held, col), 0, held - 1)
    return slot, pl.ds(pl.multiple_of(col * LANES, LANES), LANES)


def block_at(slot):
    return pl.ds(pl.multiple_of(slot * LANES, LANES), LANES)


def first_block(blocks):
    return (lax.axis_index("grp") * lax.axis_size("dev") + lax.axis_index("dev")) * blocks


def local_kernel(index_ref, tiles_ref, low_ref, high_ref, left_ref, right_ref, base_ref,
                 out_ref, near_ref, reach_ref, held_ref, sems, base_sem, side_sems):
    blocks = base_ref.shape[1] // LANES
    width = low_ref.shape[1]
    pieces = sems.shape[0]
    batch = held_ref.shape[0] // pieces
    first = first_block(blocks)

    def load(k):
        at = pl.ds(k * batch, batch)
        return pltpu.make_async_copy(tiles_ref.at[at], held_ref.at[at], sems.at[k])

    part_of = lambda k: slice(k * width, (k + 1) * width)
    right, left = [
        pltpu.make_async_copy(ref, reach_ref.at[:, part_of(2 + k)], side_sems.at[k])
        for k, ref in enumerate((right_ref, left_ref))
    ]
    right.start()
    left.start()
    start = pltpu.make_async_copy(base_ref, out_ref, base_sem)
    start.start()
    for k in range(pieces):
        load(k).start()
    for k, ref in enumerate((low_ref, high_ref)):
        reach_ref[:, part_of(k)] = ref[...]
        near_ref[:, part_of(k)] = ref[...]
    right.wait()
    near_ref[:, part_of(2)] = reach_ref[:, part_of(2)]
    left.wait()
    start.wait()

    def piece(k, carry):
        load(k).wait()
        for j in range(batch):
            t = k * batch + j
            slot, cells = place_of(index_ref, t, first, 2 * blocks)
            mine = (slot >= 0) & (slot < blocks)
            part = rows_dot(reach_ref[:, cells], held_ref[t])
            out_ref[:, block_at(jnp.clip(slot, 0, blocks - 1))] += jnp.where(mine, part, 0.0)
        return carry

    lax.fori_loop(0, pieces, piece, 0)


def last_kernel(index_ref, tiles_ref, near_ref, mid_ref, received_ref, out_ref, made_ref,
                total_ref, held_ref, sems, out_sem):
    blocks = mid_ref.shape[1] // LANES
    pieces = sems.shape[0]
    batch = held_ref.shape[0] // pieces
    first = first_block(blocks)

    def load(k):
        at = pl.ds(k * batch, batch)
        return pltpu.make_async_copy(tiles_ref.at[at], held_ref.at[at], sems.at[k])

    def store(b, carry):
        at = block_at(b)
        pltpu.make_async_copy(total_ref.at[:, at], out_ref.at[:, at], out_sem).start()
        return carry

    for k in range(pieces):
        load(k).start()
    cells_here = mid_ref.shape[1]
    total_ref[:, :cells_here] = mid_ref[...]
    total_ref[:, cells_here:] = jnp.zeros((mid_ref.shape[0], LANES), F32)
    made_ref[...] = jnp.concatenate(
        [received_ref[o] for o in range(received_ref.shape[0])], axis=1
    )
    done = 0
    for k in range(pieces):
        head = jnp.clip(index_ref[0, k * batch] - first, 0, blocks)
        lax.fori_loop(done, head, store, 0)
        done = jnp.maximum(done, head)
        load(k).wait()
        for t in range(k * batch, (k + 1) * batch):
            slot, cells = place_of(index_ref, t, first, near_ref.shape[1] // LANES)
            slot = jnp.where((slot >= 0) & (slot < blocks), slot, blocks)
            total_ref[:, block_at(slot)] += rows_dot(near_ref[:, cells], held_ref[t])
    lax.fori_loop(done, blocks, store, 0)
    pltpu.make_async_copy(total_ref.at[:, pl.ds(0, cells_here)], out_ref, out_sem).wait()


def per_device(
    tracer, tile_rows, tile_cols, tile_values, level_counts, column_owner,
    half_saturation, growth_rate, uptake, graze_preference, graze_maximum,
):
    channels, cells = tracer.shape
    tile_total, block = tile_values.shape[0], tile_values.shape[1]
    spill = tile_total // 8
    half = cells // 2
    assert half >= REACH * block and block == LANES
    devices = lax.axis_size("dev")

    source = in_hbm(tracer)
    tiles = in_hbm(tile_values)
    high = rounded(source, half, half)
    low = rounded(source, 0, half)
    left = chain_shift(high, 1)
    right = chain_shift(low, -1)

    spilled, spilled_index = pl.pallas_call(
        pack_kernel,
        out_shape=(
            jax.ShapeDtypeStruct((spill, block, block), BF16),
            jax.ShapeDtypeStruct((2, LANES), jnp.int32),
        ),
        in_specs=[HBM_SPEC, VMEM_SPEC, VMEM_SPEC, ANY_SPEC, ANY_SPEC],
        out_specs=(VMEM_SPEC, VMEM_SPEC),
        scratch_shapes=[pltpu.SemaphoreType.DMA],
        compiler_params=pltpu.CompilerParams(vmem_limit_bytes=2 << 20),
        cost_estimate=pl.CostEstimate(
            flops=0, bytes_accessed=spill * block * block * 4, transcendentals=0
        ),
    )(tiles, tile_rows[None, :], tile_cols[None, :], low, high)
    more_index = group_shift(spilled_index, -1)
    more_tiles = group_shift(spilled, -1)

    share = level_counts.shape[0] // devices
    base, send = pl.pallas_call(
        ecosystem_kernel,
        out_shape=(
            pltpu.HBM((channels, cells), F32),
            jax.ShapeDtypeStruct((devices, 1, share), F32),
        ),
        in_specs=[VMEM_SPEC] * 8 + [ANY_SPEC],
        out_specs=(HBM_SPEC, VMEM_SPEC),
        scratch_shapes=[pltpu.VMEM((channels, cells), F32)]
        + [pltpu.VMEM((cells // LANES, LANES), F32)] * 3
        + [pltpu.SemaphoreType.DMA],
        compiler_params=pltpu.CompilerParams(vmem_limit_bytes=4 << 20),
        cost_estimate=pl.CostEstimate(
            flops=cells * 30000, bytes_accessed=channels * cells * 8, transcendentals=cells
        ),
    )(
        tracer,
        level_counts[None, :],
        column_owner[None, :],
        half_saturation[None, :],
        growth_rate[None, :],
        uptake.T,
        graze_preference,
        graze_maximum[None, :],
        spilled,
    )
    received = lax.all_to_all(send, "dev", split_axis=0, concat_axis=0, tiled=True)

    index = jnp.stack([tile_rows, tile_cols])
    smem = pl.BlockSpec(memory_space=pltpu.SMEM)
    pieces = 10
    work = 2 * channels * block * block
    mid, near = pl.pallas_call(
        local_kernel,
        out_shape=(
            jax.ShapeDtypeStruct((channels, cells), F32),
            jax.ShapeDtypeStruct((channels, 3 * half), BF16),
        ),
        in_specs=[smem, HBM_SPEC] + [VMEM_SPEC] * 2 + [HBM_SPEC] * 3,
        out_specs=(VMEM_SPEC, VMEM_SPEC),
        scratch_shapes=[
            pltpu.VMEM((channels, 4 * half), BF16),
            pltpu.VMEM((tile_total, block, block), BF16),
            pltpu.SemaphoreType.DMA((pieces,)),
            pltpu.SemaphoreType.DMA,
            pltpu.SemaphoreType.DMA((2,)),
        ],
        compiler_params=pltpu.CompilerParams(vmem_limit_bytes=8 << 20),
        cost_estimate=pl.CostEstimate(
            flops=tile_total * work, bytes_accessed=tile_values.size * 2, transcendentals=0
        ),
    )(index, tiles, low, high, in_hbm(left), in_hbm(right), in_hbm(base))
    groups = 4
    updated, made = pl.pallas_call(
        last_kernel,
        out_shape=(
            jax.ShapeDtypeStruct((channels, cells), F32),
            jax.ShapeDtypeStruct((1, devices * share), F32),
        ),
        in_specs=[smem, ANY_SPEC, VMEM_SPEC, VMEM_SPEC, VMEM_SPEC],
        out_specs=(HBM_SPEC, VMEM_SPEC),
        scratch_shapes=[
            pltpu.VMEM((channels, cells + LANES), F32),
            pltpu.VMEM((spill, block, block), BF16),
            pltpu.SemaphoreType.DMA((groups,)),
            pltpu.SemaphoreType.DMA,
        ],
        compiler_params=pltpu.CompilerParams(vmem_limit_bytes=8 << 20),
        cost_estimate=pl.CostEstimate(
            flops=spill * work, bytes_accessed=channels * cells * 8, transcendentals=0
        ),
    )(more_index, more_tiles, near, mid, received)
    return updated, made.reshape(-1)


def solution(mesh):
    return jax.shard_map(
        per_device,
        mesh=mesh,
        in_specs=(
            P(None, CHAIN),
            P(CHAIN),
            P(CHAIN),
            P(CHAIN, None, None),
            P(CHAIN),
            P(CHAIN),
            P(),
            P(),
            P(),
            P(),
            P(),
        ),
        out_specs=(P(None, CHAIN), P(CHAIN)),
        check_vma=False,
    )
```

time: 64.3 us -> 56.7 us (0.88)
  waiting for transfers between devices: 19.2 us -> 10.5 us
  local copies, waits for them, and re-layouts: 8.44 us -> 1.58 us
  Pallas kernels: 17 us -> 23.6 us
  starting transfers between devices: 17.7 us -> 19.8 us
  other arithmetic: 0.67 us -> 0.01 us
    all_to_all x1, waiting for transfers between devices: 19.2 us -> 0.01 us  [per_device(): lax.all_to_all(send, 'dev', split_axis=0, concat_axis=0, tiled=True)]
    ppermute x2, waiting for transfers between devices: 0.01 us -> 10.5 us  [chain_shift(): return lax.ppermute(x, CHAIN, pairs)]
    pallas_call x5 -> x6, Pallas kernels: 17 us -> 23.6 us  [the longest x1 8.72 us: per_device(): pl.pallas_call(local_kernel, out_shape=(jax.ShapeDtypeStruct((channels, c...]
    unnamed x26 -> x24, local copies, waits for them, and re-layouts: 7.34 us -> 1.58 us
    all_to_all x1, starting transfers between devices: 8.29 us -> 10.4 us  [per_device(): lax.all_to_all(send, 'dev', split_axis=0, concat_axis=0, tiled=True)]
    all_to_all x1 -> x0, other arithmetic: 0.66 us -> none  [per_device(): lax.all_to_all(send[:, :share], 'dev', split_axis=0, concat_axis=0)]
  transfers between devices with their start and end apart: 5 -> 5, of which waited for: 1 -> 1; matrix products, arithmetic and copies ran while one was open for 3% -> 0% of each run, Pallas kernels for 10% -> 27%
where the time goes in v2:
time: 56.7 us; the launch traced here: 56.4 us
  Pallas kernels  23.6 us (42%)
  starting transfers between devices  19.8 us (35%)
  waiting for transfers between devices  10.5 us (19%)
  local copies, waits for them, and re-layouts  1.58 us (3%)
  between operations  0.89 us (2%)
    ppermute x2, waiting for transfers between devices, chain_shift(): return lax.ppermute(x, CHAIN, pairs)  10.5 us
    all_to_all x1, starting transfers between devices, per_device(): lax.all_to_all(send, 'dev', split_axis=0, concat_axis=0, tiled=True)  10.4 us
    pallas_call x1, Pallas kernels, per_device(): pl.pallas_call(local_kernel, out_shape=(jax.ShapeDtypeStruct((channels, c...  8.72 us
    ppermute x2, starting transfers between devices, chain_shift(): return lax.ppermute(x, CHAIN, pairs)  6.85 us
    pallas_call x1, Pallas kernels, per_device(): pl.pallas_call(ecosystem_kernel, out_shape=(pltpu.HBM((channels, cells),...  6.52 us
    pallas_call x1, Pallas kernels, per_device(): pl.pallas_call(last_kernel, out_shape=(jax.ShapeDtypeStruct((channels, ce...  3.77 us
    ppermute x2, starting transfers between devices, group_shift(): return lax.ppermute(x, 'dev', pairs)  2.58 us
    pallas_call x2, Pallas kernels, rounded(): pl.pallas_call(functools.partial(round_kernel, start), out_shape=jax.Shap...  2.55 us
  transfers between devices with their start and end apart: 5, of which 1 were waited for; matrix products, arithmetic and copies ran while one was open for 0% of the time, Pallas kernels for 27%

profile of v2, /device:TPU:0, one launch (start us, length us, event | category | flops | bytes accessed | tf_op | source)
XLA Modules:
  0.0 56.4 jit_solution(6638246312887487844)
XLA Ops:
  0.6 0.0 copy-start.4
  0.6 0.0 copy-start.3
  0.6 1.3 %shard_map.122.after_low_ref.low_ref = bf16[96,2048]{1,0:T(8,128)(2,1)S(1)} custom-call(f32[96,4096]{1,0:T(8,128)} %x_ref.5), custom_call_target="tpu_custom_call" | custom-call | flops 196608 | bytes 1179648 | tf_op jit(solution)/shard_map/pallas_call | solution.py:85
  1.9 1.3 %shard_map.123.after_high_ref.high_ref = bf16[96,2048]{1,0:T(8,128)(2,1)S(1)} custom-call(f32[96,4096]{1,0:T(8,128)} %x_ref.5), custom_call_target="tpu_custom_call" | custom-call | flops 196608 | bytes 1179648 | tf_op jit(solution)/shard_map/pallas_call | solution.py:85
  3.2 0.0 copy-done.4
  3.2 0.0 copy-done.3
  3.2 0.0 copy-start
  3.2 0.0 copy-start.1
  3.3 0.0 copy-start.2
  3.3 0.0 copy-start.5
  3.3 0.0 copy-start.6
  3.3 0.0 copy-start.7
  3.3 0.0 copy-start.8
  3.3 0.0 copy-start.9
  3.3 2.1 %shard_map.124 = (bf16[20,128,128]{2,1,0:T(8,128)(2,1)}, s32[2,128]{1,0:T(2,128)S(1)}) custom-call(bf16[160,128,128]{2,1,0:T(8,128)(2,1)} %tiles_ref.3, s32[1,160]{1,0:T(1,128)S(1)} %bitcast.10, s32[1,160]{1,0:T(1,128)S(1)} %bitcast.12, bf16[96,2048]{1,0:T(8,128)(2,1)S(1)} %shard_map.122.after_low_ref.low_ref, ...), custom_call_target="tpu_custom_call" | custom-call | bytes 1310720 | tf_op jit(solution)/shard_map/pallas_call | solution.py:316
  5.4 1.3 %collective-permute-start.1 = (bf16[20,128,128]{2,1,0:T(8,128)(2,1)}, bf16[20,128,128]{2,1,0:T(8,128)(2,1)}, u32[]{:S(2)}, u32[]{:S(2)}) collective-permute-start(bf16[20,128,128]{2,1,0:T(8,128)(2,1)} %get-tuple-element.11.after_ref), channel_id=1, source_target_pairs={{1,0},{2,1},{3,2},{4,3},{5,4},{6,5},{7,6},{9,8},{10,9},{11,10},{12... | collective-permute-start | bytes 1966088 | tf_op jit(solution)/shard_map/ppermute | solution.py:38
  6.7 5.6 %collective-permute-start.2 = (bf16[96,2048]{1,0:T(8,128)(2,1)S(1)}, bf16[96,2048]{1,0:T(8,128)(2,1)S(1)}, u32[]{:S(2)}, u32[]{:S(2)}) collective-permute-start(bf16[96,2048]{1,0:T(8,128)(2,1)S(1)} %shard_map.123.after_high_ref.high_ref), channel_id=1, source_target_pairs={{0,1},{1,2},{2,3},{3,4},{4,5},{5,6},{6,7},{7,8},{8,9},{9,10},{10,1... | collective-permute-start | bytes 1179656 | tf_op jit(solution)/shard_map/ppermute | solution.py:32
  12.3 1.3 %collective-permute-start.3 = (bf16[96,2048]{1,0:T(8,128)(2,1)S(1)}, bf16[96,2048]{1,0:T(8,128)(2,1)S(1)}, u32[]{:S(2)}, u32[]{:S(2)}) collective-permute-start(bf16[96,2048]{1,0:T(8,128)(2,1)S(1)} %shard_map.122.after_low_ref.low_ref), channel_id=1, source_target_pairs={{1,0},{2,1},{3,2},{4,3},{5,4},{6,5},{7,6},{8,7},{9,8},{10,9},{11,1... | collective-permute-start | bytes 1179656 | tf_op jit(solution)/shard_map/ppermute | solution.py:32
  13.6 1.3 %collective-permute-start = (s32[2,128]{1,0:T(2,128)S(1)}, s32[2,128]{1,0:T(2,128)S(1)}, u32[]{:S(2)}, u32[]{:S(2)}) collective-permute-start(s32[2,128]{1,0:T(2,128)S(1)} %get-tuple-element.10), channel_id=1, source_target_pairs={{1,0},{2,1},{3,2},{4,3},{5,4},{6,5},{7,6},{9,8},{10,9},{11,10},{12... | collective-permute-start | bytes 3080 | tf_op jit(solution)/shard_map/ppermute | solution.py:38
  14.9 0.0 copy-done
  14.9 0.0 copy-done.1
  14.9 0.0 copy-done.2
  14.9 0.0 copy-done.5
  14.9 0.0 copy-done.6
  14.9 0.0 copy-done.7
  14.9 0.0 copy-done.8
  14.9 0.0 copy-done.9
  14.9 6.5 %shard_map.125 = (f32[96,4096]{1,0:T(8,128)}, f32[8,1,16]{2,1,0:T(1,128)}) custom-call(f32[96,4096]{1,0:T(8,128)S(1)} %copy-done, s32[1,128]{1,0:T(1,128)S(1)} %bitcast.14, s32[1,128]{1,0:T(1,128)S(1)} %bitcast.15, f32[1,16]{1,0:T(1,128)S(1)} %bitcast.16, f32[1,64]{1,0:T(1,128)S(1)} %bitcast.17, f32[16,64]{1,0:T(8,128)S(1)} %bitcast.9, ...), custom_call_target="tpu_custom_call" | custom-call | flops 122880000 | bytes 3145728 | tf_op jit(solution)/shard_map/pallas_call | solution.py:334
  21.5 10.4 %all-to-all-start = ((f32[8,1,16]{2,1,0:T(1,128)}), f32[8,1,16]{2,1,0:T(1,128)S(1)}, u32[]{:S(2)}, u32[]{:S(2)}) async-start(f32[8,1,16]{2,1,0:T(1,128)} %get-tuple-element.15), calls=%async_computation | async-start | bytes 8192 | tf_op jit(solution)/shard_map/all_to_all | solution.py:360
  31.8 10.5 %collective-permute-done.2.left_ref = bf16[96,2048]{1,0:T(8,128)(2,1)S(1)} collective-permute-done((bf16[96,2048]{1,0:T(8,128)(2,1)S(1)}, bf16[96,2048]{1,0:T(8,128)(2,1)S(1)}, u32[]{:S(2)}, u32[]{:S(2)}) %collective-permute-start.2) | collective-permute-done | bytes 393248 | tf_op jit(solution)/shard_map/ppermute | solution.py:32
  42.3 0.0 copy-start.10
  42.3 0.0 collective-permute-done.3.right_ref
  42.3 0.7 %copy-done.10 = bf16[96,2048]{1,0:T(8,128)(2,1)} copy-done((bf16[96,2048]{1,0:T(8,128)(2,1)}, bf16[96,2048]{1,0:T(8,128)(2,1)S(1)}, u32[]{:S(2)}) %copy-start.10) | copy-done | bytes 393240
  43.0 0.0 copy-start.11
  43.0 0.8 %copy-done.11 = bf16[96,2048]{1,0:T(8,128)(2,1)} copy-done((bf16[96,2048]{1,0:T(8,128)(2,1)}, bf16[96,2048]{1,0:T(8,128)(2,1)S(1)}, u32[]{:S(2)}) %copy-start.11) | copy-done | bytes 393240
  43.8 8.7 %shard_map.126 = (f32[96,4096]{1,0:T(8,128)S(1)}, bf16[96,6144]{1,0:T(8,128)(2,1)S(1)}) custom-call(s32[2,160]{1,0:T(2,128)S(1)} %pad_add_fusion.index_ref, bf16[160,128,128]{2,1,0:T(8,128)(2,1)} %tiles_ref.3, bf16[96,2048]{1,0:T(8,128)(2,1)S(1)} %shard_map.122.after_low_ref.low_ref, bf16[96,2048]{1,0:T(8,128)(2,1)S(1)} %shard_map.123.after_high_ref.high_ref, ...), custom_call_target="tpu_custom_call" | custom-call | flops 503316480 | bytes 5242880 | tf_op jit(solution)/shard_map/pallas_call | solution.py:366
  52.6 0.0 all-to-all-done.received_ref
  52.6 0.0 collective-permute-done.index_ref
  52.6 0.0 collective-permute-done.1.tiles_ref
  52.6 3.8 %shard_map.127 = (f32[96,4096]{1,0:T(8,128)}, f32[1,128]{1,0:T(1,128)}) custom-call(s32[2,128]{1,0:T(2,128)S(1)} %collective-permute-done.index_ref, bf16[20,128,128]{2,1,0:T(8,128)(2,1)} %collective-permute-done.1.tiles_ref, bf16[96,6144]{1,0:T(8,128)(2,1)S(1)} %get-tuple-element.13.near_ref, f32[96,4096]{1,0:T(8,128)S(1)} %get-tuple-element.14.mid_ref, ...), custom_call_target="tpu_custom_call" | custom-call | flops 62914560 | bytes 3145728 | tf_op jit(solution)/shard_map/pallas_call | solution.py:387
  (1 shorter events, 0.0 us)
Async XLA Ops:
  0.6 2.6 %copy-start.4 = (s32[160]{0:T(256)S(1)}, s32[160]{0:T(256)}, u32[]{:S(2)}) copy-start(s32[160]{0:T(256)} %param.13) | copy-start | bytes 1924
  0.6 2.6 %copy-start.3 = (s32[160]{0:T(256)S(1)}, s32[160]{0:T(256)}, u32[]{:S(2)}) copy-start(s32[160]{0:T(256)} %param.12) | copy-start | bytes 1924
  3.2 11.6 %copy-start = (f32[96,4096]{1,0:T(8,128)S(1)}, f32[96,4096]{1,0:T(8,128)}, u32[]{:S(2)}) copy-start(f32[96,4096]{1,0:T(8,128)} %x_ref.5) | copy-start | bytes 4718596
  3.2 11.6 %copy-start.1 = (f32[64,64]{1,0:T(8,128)S(1)}, f32[64,64]{1,0:T(8,128)}, u32[]{:S(2)}) copy-start(f32[64,64]{1,0:T(8,128)} %prefer_ref.1) | copy-start | bytes 49156
  3.3 11.6 %copy-start.2 = (f32[64,16]{0,1:T(8,128)S(1)}, f32[64,16]{0,1:T(8,128)}, u32[]{:S(2)}) copy-start(f32[64,16]{0,1:T(8,128)} %param.19) | copy-start | bytes 12292
  3.3 11.6 %copy-start.5 = (s32[128]{0:T(128)S(1)}, s32[128]{0:T(128)}, u32[]{:S(2)}) copy-start(s32[128]{0:T(128)} %param.15) | copy-start | bytes 1540
  3.3 11.6 %copy-start.6 = (s32[128]{0:T(128)S(1)}, s32[128]{0:T(128)}, u32[]{:S(2)}) copy-start(s32[128]{0:T(128)} %param.16) | copy-start | bytes 1540
  3.3 11.6 %copy-start.7 = (f32[16]{0:T(128)S(1)}, f32[16]{0:T(128)}, u32[]{:S(2)}) copy-start(f32[16]{0:T(128)} %param.17) | copy-start | bytes 196
  3.3 11.6 %copy-start.8 = (f32[64]{0:T(128)S(1)}, f32[64]{0:T(128)}, u32[]{:S(2)}) copy-start(f32[64]{0:T(128)} %param.18) | copy-start | bytes 772
  3.3 11.6 %copy-start.9 = (f32[64]{0:T(128)S(1)}, f32[64]{0:T(128)}, u32[]{:S(2)}) copy-start(f32[64]{0:T(128)} %param.21) | copy-start | bytes 772
  5.4 47.2 %collective-permute-start.1 = (bf16[20,128,128]{2,1,0:T(8,128)(2,1)}, bf16[20,128,128]{2,1,0:T(8,128)(2,1)}, u32[]{:S(2)}, u32[]{:S(2)}) collective-permute-start(bf16[20,128,128]{2,1,0:T(8,128)(2,1)} %get-tuple-element.11.after_ref), channel_id=1, source_target_pairs={{1,0},{2,1},{3,2},{4,3},{5,4},{6,5},{7,6},{9,8},{10,9},{11,10},{12... | collective-permute-start | bytes 1966088 | tf_op jit(solution)/shard_map/ppermute | solution.py:38
  6.7 35.6 %collective-permute-start.2 = (bf16[96,2048]{1,0:T(8,128)(2,1)S(1)}, bf16[96,2048]{1,0:T(8,128)(2,1)S(1)}, u32[]{:S(2)}, u32[]{:S(2)}) collective-permute-start(bf16[96,2048]{1,0:T(8,128)(2,1)S(1)} %shard_map.123.after_high_ref.high_ref), channel_id=1, source_target_pairs={{0,1},{1,2},{2,3},{3,4},{4,5},{5,6},{6,7},{7,8},{8,9},{9,10},{10,1... | collective-permute-start | bytes 1179656 | tf_op jit(solution)/shard_map/ppermute | solution.py:32
  12.3 30.0 %collective-permute-start.3 = (bf16[96,2048]{1,0:T(8,128)(2,1)S(1)}, bf16[96,2048]{1,0:T(8,128)(2,1)S(1)}, u32[]{:S(2)}, u32[]{:S(2)}) collective-permute-start(bf16[96,2048]{1,0:T(8,128)(2,1)S(1)} %shard_map.122.after_low_ref.low_ref), channel_id=1, source_target_pairs={{1,0},{2,1},{3,2},{4,3},{5,4},{6,5},{7,6},{8,7},{9,8},{10,9},{11,1... | collective-permute-start | bytes 1179656 | tf_op jit(solution)/shard_map/ppermute | solution.py:32
  13.6 39.0 %collective-permute-start = (s32[2,128]{1,0:T(2,128)S(1)}, s32[2,128]{1,0:T(2,128)S(1)}, u32[]{:S(2)}, u32[]{:S(2)}) collective-permute-start(s32[2,128]{1,0:T(2,128)S(1)} %get-tuple-element.10), channel_id=1, source_target_pairs={{1,0},{2,1},{3,2},{4,3},{5,4},{6,5},{7,6},{9,8},{10,9},{11,10},{12... | collective-permute-start | bytes 3080 | tf_op jit(solution)/shard_map/ppermute | solution.py:38
  21.5 31.1 %all-to-all-start = ((f32[8,1,16]{2,1,0:T(1,128)}), f32[8,1,16]{2,1,0:T(1,128)S(1)}, u32[]{:S(2)}, u32[]{:S(2)}) async-start(f32[8,1,16]{2,1,0:T(1,128)} %get-tuple-element.15), calls=%async_computation | async-start | bytes 8192 | tf_op jit(solution)/shard_map/all_to_all | solution.py:360
  42.3 0.7 %copy-start.10 = (bf16[96,2048]{1,0:T(8,128)(2,1)}, bf16[96,2048]{1,0:T(8,128)(2,1)S(1)}, u32[]{:S(2)}) copy-start(bf16[96,2048]{1,0:T(8,128)(2,1)S(1)} %collective-permute-done.2.left_ref) | copy-start | bytes 1179652
  43.0 0.8 %copy-start.11 = (bf16[96,2048]{1,0:T(8,128)(2,1)}, bf16[96,2048]{1,0:T(8,128)(2,1)S(1)}, u32[]{:S(2)}) copy-start(bf16[96,2048]{1,0:T(8,128)(2,1)S(1)} %collective-permute-done.3.right_ref) | copy-start | bytes 1179652

commit v3 on v2

v3 whole, which is shorter than its diff:
```python
import functools

import jax
import jax.numpy as jnp
from jax import lax
from jax.experimental import pallas as pl
from jax.experimental.pallas import tpu as pltpu
from jax.sharding import PartitionSpec as P

NUT = 16
PLK = 64
LEV = 32
REACH = 16
LANES = 128
CHUNK = 256
SPAN = 512

HIGHEST = lax.Precision.HIGHEST
WATER_DECAY = 0.03
SHADE_DECAY = 0.05
EFFICIENCY = 0.3
MORTALITY = 0.1
REMINERAL = 0.2
TIMESTEP = 0.5
F32 = jnp.float32
BF16 = jnp.bfloat16
CHAIN = ("grp", "dev")


def chain_shift(x, step):
    count = lax.axis_size(CHAIN)
    pairs = [(i, i + step) for i in range(count) if 0 <= i + step < count]
    return lax.ppermute(x, CHAIN, pairs)


def group_shift(x, step):
    count = lax.axis_size("dev")
    pairs = [(i, i + step) for i in range(count) if 0 <= i + step < count]
    return lax.ppermute(x, "dev", pairs)


def iota(shape, dim):
    return lax.broadcasted_iota(jnp.int32, shape, dim)


def rows_dot(a, b, precision=None):
    return lax.dot_general(
        a, b, (((1,), (1,)), ((), ())), precision=precision, preferred_element_type=F32
    )


def dot(a, b, precision=None):
    return jnp.dot(a, b, precision=precision, preferred_element_type=F32)


def in_hbm(x):
    return pltpu.with_memory_space_constraint(x, pltpu.HBM)


VMEM_SPEC = pl.BlockSpec(memory_space=pltpu.VMEM)
HBM_SPEC = pl.BlockSpec(memory_space=pltpu.HBM)
ANY_SPEC = pl.BlockSpec(memory_space=pl.ANY)


def round_kernel(start, x_ref, out_ref, held_ref, sems):
    pieces = sems.shape[0]
    width = out_ref.shape[1] // pieces

    def load(k):
        return pltpu.make_async_copy(
            x_ref.at[:, pl.ds(start + k * width, width)],
            held_ref.at[:, pl.ds(k * width, width)],
            sems.at[k],
        )

    for k in range(pieces):
        load(k).start()
    for k in range(pieces):
        load(k).wait()
        at = slice(k * width, (k + 1) * width)
        out_ref[:, at] = held_ref[:, at].astype(BF16)


def rounded(x, start, width, pieces=4):
    rows = x.shape[0]
    return pl.pallas_call(
        functools.partial(round_kernel, start),
        out_shape=jax.ShapeDtypeStruct((rows, width), BF16),
        in_specs=[HBM_SPEC],
        out_specs=VMEM_SPEC,
        scratch_shapes=[pltpu.VMEM((rows, width), F32), pltpu.SemaphoreType.DMA((pieces,))],
        compiler_params=pltpu.CompilerParams(vmem_limit_bytes=4 << 20),
        cost_estimate=pl.CostEstimate(
            flops=rows * width, bytes_accessed=rows * width * 6, transcendentals=0
        ),
    )(x)


def exact_dot(a, ones):
    n = a.shape[0]
    parts, rest = [], a
    for _ in range(3):
        part = rest.astype(BF16)
        parts.append(part.astype(F32))
        rest = rest - parts[-1]
    out = dot(jnp.concatenate(parts, axis=0).astype(BF16), ones)
    return out[:n] + out[n : 2 * n] + out[2 * n :]


def upright(ref):
    n = ref.shape[1]
    return jnp.sum(
        jnp.where(iota((n, n), 0) == iota((n, n), 1), ref[...], 0.0), axis=1, keepdims=True
    )


def plankton_sent(low_ref, high_ref, c, width):
    half = low_ref.shape[1]
    start = c * width
    ref, at = (low_ref, start) if start < half else (high_ref, start - half)
    return ref[NUT : NUT + PLK, at : at + width]


def produce_kernel(
    x_ref, low_ref, high_ref, level_ref, owner_ref, half_ref, rate_ref, uptake_ref,
    rows_ref, cols_ref, tiles_ref,
    send_ref, lead_ref, rest_ref, light_ref, wet_ref, index_ref, sums_ref, made_ref, held_ref,
    few_ref, more_sem, few_sem,
):
    few = pltpu.make_async_copy(x_ref.at[pl.ds(0, NUT)], few_ref, few_sem)
    few.start()
    lead = lead_ref.shape[0]
    spill = lead + rest_ref.shape[0]
    pack = pltpu.make_async_copy(tiles_ref.at[pl.ds(0, spill)], held_ref, more_sem)
    pack.start()
    cells = x_ref.shape[1]
    blocks = cells // LANES
    slot, col = places(
        rows_ref[...], cols_ref[...], first_block(blocks), blocks, 2 * blocks
    )
    index_ref[0:1, :] = slot
    index_ref[1:2, :] = col
    per_block = LANES // LEV
    columns = level_ref.shape[1]
    devices = send_ref.shape[0]
    share = columns // devices

    half = upright(half_ref)
    weight = jnp.concatenate(
        [uptake_ref[...] * rate_ref[...], jnp.ones((NUT, PLK), F32)], axis=0
    ).astype(BF16)
    few.wait()
    for c in range(cells // SPAN):
        both = dot(weight, plankton_sent(low_ref, high_ref, c, SPAN))
        nutrient = few_ref[:, c * SPAN : (c + 1) * SPAN]
        monod = nutrient / (nutrient + half)
        total = both[NUT : NUT + 1]
        taken = jnp.sum(monod * both[:NUT], axis=0, keepdims=True)
        for s in range(SPAN // LANES):
            row = c * (SPAN // LANES) + s
            sums_ref[row : row + 1, :] = total[:, s * LANES : (s + 1) * LANES]
            made_ref[row : row + 1, :] = taken[:, s * LANES : (s + 1) * LANES]

    pack.wait()
    packs = [
        pltpu.make_async_copy(held_ref.at[pl.ds(0, lead)], lead_ref, more_sem),
        pltpu.make_async_copy(held_ref.at[pl.ds(lead, spill - lead)], rest_ref, few_sem),
    ]
    for pack in packs:
        pack.start()

    mine = iota((blocks, columns), 1) // per_block == iota((blocks, columns), 0)
    spread = iota((columns, LANES), 0) % per_block == iota((columns, LANES), 1) // LEV
    gather = iota((LANES, columns), 1) % per_block == iota((LANES, columns), 0) // LEV
    levels = level_ref[...].astype(F32)
    counts = dot(jnp.where(mine, levels, 0.0).astype(BF16), spread.astype(BF16))
    depth = (iota((blocks, LANES), 1) % LEV).astype(F32)
    wet = (depth < counts).astype(F32)
    wet_ref[...] = wet
    upper, lower = iota((LANES, LANES), 0), iota((LANES, LANES), 1)
    above = ((upper // LEV == lower // LEV) & (upper < lower)).astype(BF16)
    shading = exact_dot(sums_ref[...] / PLK * wet, above)
    light = jnp.exp(-WATER_DECAY * depth - SHADE_DECAY * shading)
    light_ref[...] = light

    by_column = exact_dot(light * made_ref[...] / PLK * wet, gather.astype(BF16))
    production = jnp.sum(jnp.where(mine, by_column, 0.0), axis=0, keepdims=True)
    owned = owner_ref[...] == iota((devices, columns), 0)
    before = (iota((columns, columns), 0) < iota((columns, columns), 1)).astype(BF16)
    earlier = dot(owned.astype(BF16), before)
    rank = jnp.sum(jnp.where(owned, earlier, 0.0), axis=0, keepdims=True).astype(jnp.int32)
    place = (rank == iota((LANES, columns), 0)).astype(F32)
    sorted_sums = rows_dot(jnp.where(owned, production, 0.0), place, HIGHEST)
    lane = iota((1, LANES), 1)
    rows = pltpu.roll(rows_ref[:, :LANES].astype(F32), share, 1)
    cols = pltpu.roll(cols_ref[:, :LANES].astype(F32), share + spill, 1)
    index = jnp.where(lane < share + spill, rows, cols)
    for o in range(devices):
        send_ref[o] = jnp.where(lane < share, sorted_sums[o : o + 1, :], index)
    for pack in packs:
        pack.wait()


def ecosystem_kernel(
    x_ref, low_ref, high_ref, light_ref, wet_ref, half_ref, rate_ref, uptake_ref, prefer_ref,
    graze_ref,
    far_ref, base_ref, held_ref, sem, sems,
):
    cells = x_ref.shape[1]
    pieces = sems.shape[0]
    piece = cells // pieces

    def load(k):
        at = pl.ds(k * piece, piece)
        return pltpu.make_async_copy(x_ref.at[:, at], held_ref.at[:, at], sems.at[k])

    for k in range(pieces):
        load(k).start()
    half = upright(half_ref)
    rate = upright(rate_ref)
    most = upright(graze_ref)
    prefer = prefer_ref[...]
    uptake_b = uptake_ref[...].T.astype(BF16)
    quarter = (iota((NUT, PLK), 1) // (PLK // NUT) == iota((NUT, PLK), 0)).astype(F32)
    first = jnp.concatenate([prefer, uptake_ref[...] * rate_ref[...]], axis=0).astype(BF16)
    second = jnp.concatenate(
        [
            jnp.concatenate([prefer.T, jnp.zeros((PLK, 2 * PLK), F32)], axis=1),
            jnp.concatenate([jnp.zeros((NUT, PLK), F32), quarter, quarter], axis=1),
        ],
        axis=0,
    ).astype(BF16)
    span = CHUNK // LANES

    def row_of(ref, c):
        return jnp.concatenate([ref[c * span + s : c * span + s + 1, :] for s in range(span)], axis=1)

    for c in range(cells // CHUNK):
        if c * CHUNK % piece == 0:
            load(c * CHUNK // piece).wait()
        plankton_b = plankton_sent(low_ref, high_ref, c, CHUNK)
        at = slice(c * CHUNK, (c + 1) * CHUNK)
        nutrient = held_ref[:NUT, at]
        plankton = held_ref[NUT : NUT + PLK, at]
        detritus = held_ref[NUT + PLK :, at]
        sun = row_of(light_ref, c)
        mask = row_of(wet_ref, c)
        both = dot(first, plankton_b)
        food, drawn = both[:PLK], both[PLK:]
        monod = nutrient / (nutrient + half)
        limitation = dot(uptake_b, monod.astype(BF16))
        growth = rate * sun * plankton * limitation
        graze = most * plankton / (1.0 + food)
        eaten = graze * food
        waste = (1.0 - EFFICIENCY) * eaten + MORTALITY * plankton
        waste_high = waste.astype(BF16)
        waste_low = (waste - waste_high.astype(F32)).astype(BF16)
        both = dot(second, jnp.concatenate([graze.astype(BF16), waste_high, waste_low], axis=0))
        lost, fallen = both[:PLK], both[PLK:]
        d_plankton = growth - plankton * lost + EFFICIENCY * eaten - MORTALITY * plankton
        d_nutrient = REMINERAL * detritus - monod * sun * drawn
        d_detritus = fallen - REMINERAL * detritus
        scale = TIMESTEP * mask
        base_ref[:NUT, at] = nutrient + scale * d_nutrient
        base_ref[NUT : NUT + PLK, at] = plankton + scale * d_plankton
        base_ref[NUT + PLK :, at] = detritus + scale * d_detritus
        if c % 4 == 3:
            done = pl.ds((c - 3) * CHUNK, 4 * CHUNK)
            pltpu.make_async_copy(base_ref.at[:, done], far_ref.at[:, done], sem).start()
    pltpu.make_async_copy(base_ref, far_ref, sem).wait()


def places(rows, cols, first, blocks, held):
    slot, col = rows - first, cols - first
    slot = jnp.where((slot >= 0) & (slot < blocks), slot, blocks)
    return slot, jnp.clip(jnp.where(col < 0, col + held, col), 0, held - 1)


def block_at(slot):
    return pl.ds(pl.multiple_of(slot * LANES, LANES), LANES)


def first_block(blocks):
    return (lax.axis_index("grp") * lax.axis_size("dev") + lax.axis_index("dev")) * blocks


def local_kernel(index_ref, tiles_ref, low_ref, high_ref, left_ref, right_ref, base_ref,
                 received_ref, out_ref, picked_ref, slot_ref, made_ref,
                 reach_ref, held_ref, vector_ref, far_ref, sems, base_sem, far_sem):
    cells = base_ref.shape[1]
    blocks = cells // LANES
    width = low_ref.shape[1]
    pieces = sems.shape[0]
    batch = held_ref.shape[0] // pieces
    spill = picked_ref.shape[0]
    devices = received_ref.shape[0]
    share = made_ref.shape[1] // devices

    def load(k):
        at = pl.ds(k * batch, batch)
        return pltpu.make_async_copy(tiles_ref.at[at], held_ref.at[at], sems.at[k])

    me = lax.axis_index("dev")
    row = received_ref[jnp.minimum(me + 1, devices - 1)]
    row = jnp.where(me + 1 < devices, row, -1.0).astype(jnp.int32)
    slot, col = places(row, row, first_block(blocks), blocks, 2 * blocks)
    vector_ref[...] = jnp.where(iota(row.shape, 1) < share + spill, slot, col)
    move = pltpu.make_async_copy(vector_ref, far_ref, far_sem)
    move.start()
    slot_ref[...] = pltpu.roll(slot, LANES - share, 1)
    made_ref[...] = jnp.concatenate(
        [received_ref[o][:, :share] for o in range(devices)], axis=1
    )
    part_of = lambda k: slice(k * width, (k + 1) * width)
    load(0).start()
    start = pltpu.make_async_copy(base_ref, out_ref.at[:, pl.ds(0, cells)], base_sem)
    start.start()
    for k in range(1, pieces):
        load(k).start()
    for k, ref in enumerate((low_ref, high_ref, right_ref, left_ref)):
        reach_ref[:, part_of(k)] = ref[...]
    move.wait()
    for t in range(spill):
        picked_ref[t] = reach_ref[:, block_at(far_ref[0, share + spill + t])]
    out_ref[:, cells:] = jnp.zeros((out_ref.shape[0], LANES), F32)
    start.wait()

    def piece(k, carry):
        load(k).wait()
        for j in range(batch):
            t = k * batch + j
            out_ref[:, block_at(index_ref[0, t])] += rows_dot(
                reach_ref[:, block_at(index_ref[1, t])], held_ref[t]
            )
        return carry

    lax.fori_loop(0, pieces, piece, 0)


def last_kernel(slot_ref, lead_ref, rest_ref, picked_ref, mid_ref, out_ref, total_ref, out_sem):
    cells = out_ref.shape[1]
    blocks = cells // LANES

    def store(b, carry):
        at = block_at(b)
        pltpu.make_async_copy(total_ref.at[:, at], out_ref.at[:, at], out_sem).start()
        return carry

    total_ref[...] = mid_ref[...]
    done, before = 0, 0
    for ref in (lead_ref, rest_ref):
        head = slot_ref[0, before]
        lax.fori_loop(done, head, store, 0)
        done = jnp.maximum(done, head)
        for j in range(ref.shape[0]):
            t = before + j
            total_ref[:, block_at(slot_ref[0, t])] += rows_dot(picked_ref[t], ref[j])
        before += ref.shape[0]
    lax.fori_loop(done, blocks, store, 0)
    pltpu.make_async_copy(total_ref.at[:, pl.ds(0, cells)], out_ref, out_sem).wait()


def per_device(
    tracer, tile_rows, tile_cols, tile_values, level_counts, column_owner,
    half_saturation, growth_rate, uptake, graze_preference, graze_maximum,
):
    channels, cells = tracer.shape
    tile_total, block = tile_values.shape[0], tile_values.shape[1]
    spill = tile_total // 8
    half = cells // 2
    assert half >= REACH * block and block == LANES
    assert level_counts.shape[0] // lax.axis_size("dev") + 2 * spill <= LANES
    devices = lax.axis_size("dev")

    source = in_hbm(tracer)
    tiles = in_hbm(tile_values)
    high = rounded(source, half, half)
    low = rounded(source, 0, half)
    left = chain_shift(high, 1)
    right = chain_shift(low, -1)

    share = level_counts.shape[0] // devices
    blocks = cells // block
    lead = spill // 4
    send, spilled_lead, spilled_rest, light, wet, index = pl.pallas_call(
        produce_kernel,
        out_shape=(
            jax.ShapeDtypeStruct((devices, 1, LANES), F32),
            pltpu.HBM((lead, block, block), BF16),
            pltpu.HBM((spill - lead, block, block), BF16),
            jax.ShapeDtypeStruct((blocks, LANES), F32),
            jax.ShapeDtypeStruct((blocks, LANES), F32),
            jax.ShapeDtypeStruct((2, tile_total), jnp.int32),
        ),
        in_specs=[HBM_SPEC] + [VMEM_SPEC] * 9 + [HBM_SPEC],
        out_specs=(VMEM_SPEC, HBM_SPEC, HBM_SPEC) + (VMEM_SPEC,) * 3,
        scratch_shapes=[
            pltpu.VMEM((blocks, LANES), F32),
            pltpu.VMEM((blocks, LANES), F32),
            pltpu.VMEM((spill, block, block), BF16),
            pltpu.VMEM((NUT, cells), F32),
            pltpu.SemaphoreType.DMA,
            pltpu.SemaphoreType.DMA,
        ],
        compiler_params=pltpu.CompilerParams(vmem_limit_bytes=4 << 20),
        cost_estimate=pl.CostEstimate(
            flops=cells * 8000, bytes_accessed=channels * cells * 4, transcendentals=cells
        ),
    )(
        source,
        low,
        high,
        level_counts[None, :],
        column_owner[None, :],
        half_saturation[None, :],
        growth_rate[None, :],
        uptake.T,
        tile_rows[None, :],
        tile_cols[None, :],
        tiles,
    )
    received = lax.all_to_all(send, "dev", split_axis=0, concat_axis=0, tiled=True)

    lead_tiles = group_shift(spilled_lead, -1)
    rest_tiles = group_shift(spilled_rest, -1)
    base = pl.pallas_call(
        ecosystem_kernel,
        out_shape=pltpu.HBM((channels, cells), F32),
        in_specs=[HBM_SPEC] + [VMEM_SPEC] * 9,
        out_specs=HBM_SPEC,
        scratch_shapes=[pltpu.VMEM((channels, cells), F32)] * 2
        + [pltpu.SemaphoreType.DMA, pltpu.SemaphoreType.DMA((4,))],
        compiler_params=pltpu.CompilerParams(vmem_limit_bytes=4 << 20),
        cost_estimate=pl.CostEstimate(
            flops=cells * 30000, bytes_accessed=channels * cells * 8, transcendentals=0
        ),
    )(
        source,
        low,
        high,
        light,
        wet,
        half_saturation[None, :],
        growth_rate[None, :],
        uptake.T,
        graze_preference,
        graze_maximum[None, :],
    )

    smem = pl.BlockSpec(memory_space=pltpu.SMEM)
    pieces = 10
    work = 2 * channels * block * block
    mid, picked, slots, made = pl.pallas_call(
        local_kernel,
        out_shape=(
            jax.ShapeDtypeStruct((channels, cells + LANES), F32),
            jax.ShapeDtypeStruct((spill, channels, block), BF16),
            jax.ShapeDtypeStruct((1, LANES), jnp.int32),
            jax.ShapeDtypeStruct((1, devices * share), F32),
        ),
        in_specs=[smem, HBM_SPEC] + [VMEM_SPEC] * 4 + [HBM_SPEC, VMEM_SPEC],
        out_specs=(VMEM_SPEC,) * 4,
        scratch_shapes=[
            pltpu.VMEM((channels, 4 * half), BF16),
            pltpu.VMEM((tile_total, block, block), BF16),
            pltpu.VMEM((1, LANES), jnp.int32),
            pltpu.SMEM((1, LANES), jnp.int32),
            pltpu.SemaphoreType.DMA((pieces,)),
            pltpu.SemaphoreType.DMA,
            pltpu.SemaphoreType.DMA,
        ],
        compiler_params=pltpu.CompilerParams(vmem_limit_bytes=10 << 20),
        cost_estimate=pl.CostEstimate(
            flops=tile_total * work, bytes_accessed=tile_values.size * 2, transcendentals=0
        ),
    )(index, tiles, low, high, left, right, in_hbm(base), received)
    updated = pl.pallas_call(
        last_kernel,
        out_shape=jax.ShapeDtypeStruct((channels, cells), F32),
        in_specs=[smem] + [VMEM_SPEC] * 4,
        out_specs=HBM_SPEC,
        scratch_shapes=[
            pltpu.VMEM((channels, cells + LANES), F32),
            pltpu.SemaphoreType.DMA,
        ],
        compiler_params=pltpu.CompilerParams(vmem_limit_bytes=6 << 20),
        cost_estimate=pl.CostEstimate(
            flops=spill * work, bytes_accessed=channels * cells * 8, transcendentals=0
        ),
    )(slots, lead_tiles, rest_tiles, picked, mid)
    return updated, made.reshape(-1)


def solution(mesh):
    return jax.shard_map(
        per_device,
        mesh=mesh,
        in_specs=(
            P(None, CHAIN),
            P(CHAIN),
            P(CHAIN),
            P(CHAIN, None, None),
            P(CHAIN),
            P(CHAIN),
            P(),
            P(),
            P(),
            P(),
            P(),
        ),
        out_specs=(P(None, CHAIN), P(CHAIN)),
        check_vma=False,
    )
```

time: 56.7 us -> 54.9 us (0.968)
  waiting for transfers between devices: 10.5 us -> 13.4 us
  Pallas kernels: 23.6 us -> 20.9 us
  local copies, waits for them, and re-layouts: 1.58 us -> 0.04 us
    all_to_all x1, waiting for transfers between devices: 0.01 us -> 13.4 us  [per_device(): lax.all_to_all(send, 'dev', split_axis=0, concat_axis=0, tiled=True)]
    ppermute x2, waiting for transfers between devices: 10.5 us -> 0.01 us  [chain_shift(): return lax.ppermute(x, CHAIN, pairs)]
    pallas_call x3, Pallas kernels: 12.4 us -> 9.53 us  [the longest x1 4.02 us: per_device(): pl.pallas_call(ecosystem_kernel, out_shape=pltpu.HBM((channels, cells), F...]
    unnamed x24 -> x18, local copies, waits for them, and re-layouts: 1.58 us -> 0.04 us
    all_to_all x1, starting transfers between devices: 10.4 us -> 9.26 us  [per_device(): lax.all_to_all(send, 'dev', split_axis=0, concat_axis=0, tiled=True)]
    ppermute x2, starting transfers between devices: 6.85 us -> 7.47 us  [chain_shift(): return lax.ppermute(x, CHAIN, pairs)]
  transfers between devices with their start and end apart: 5 -> 5, of which waited for: 1 -> 1; matrix products, arithmetic and copies ran while one was open for 0% -> 0% of each run, Pallas kernels for 27% -> 24%
where the time goes in v3:
time: 54.9 us; the launch traced here: 54.6 us
  Pallas kernels  20.9 us (38%)
  starting transfers between devices  19.3 us (35%)
  waiting for transfers between devices  13.4 us (24%)
  between operations  0.86 us (2%)
    all_to_all x1, waiting for transfers between devices, per_device(): lax.all_to_all(send, 'dev', split_axis=0, concat_axis=0, tiled=True)  13.4 us
    all_to_all x1, starting transfers between devices, per_device(): lax.all_to_all(send, 'dev', split_axis=0, concat_axis=0, tiled=True)  9.26 us
    pallas_call x1, Pallas kernels, per_device(): pl.pallas_call(local_kernel, out_shape=(jax.ShapeDtypeStruct((channels, c...  8.82 us
    ppermute x2, starting transfers between devices, chain_shift(): return lax.ppermute(x, CHAIN, pairs)  7.47 us
    pallas_call x1, Pallas kernels, per_device(): pl.pallas_call(ecosystem_kernel, out_shape=pltpu.HBM((channels, cells), F...  4.02 us
    pallas_call x1, Pallas kernels, per_device(): pl.pallas_call(produce_kernel, out_shape=(jax.ShapeDtypeStruct((devices,...  3.18 us
    ppermute x2, starting transfers between devices, group_shift(): return lax.ppermute(x, 'dev', pairs)  2.58 us
    pallas_call x2, Pallas kernels, rounded(): pl.pallas_call(functools.partial(round_kernel, start), out_shape=jax.Shap...  2.57 us
  transfers between devices with their start and end apart: 5, of which 1 were waited for; matrix products, arithmetic and copies ran while one was open for 0% of the time, Pallas kernels for 24%

profile of v3, /device:TPU:0, one launch (start us, length us, event | category | flops | bytes accessed | tf_op | source)
XLA Modules:
  0.0 54.6 jit_solution(4945288723844663617)
XLA Ops:
  0.6 0.0 copy-start.1
  0.6 0.0 copy-start.3
  0.7 0.0 copy-start.2
  0.7 0.0 copy-start.7
  0.7 0.0 copy-start.6
  0.7 0.0 copy-start.5
  0.7 0.0 copy-start.4
  0.7 1.3 %shard_map.123.high_ref = bf16[96,2048]{1,0:T(8,128)(2,1)S(1)} custom-call(f32[96,4096]{1,0:T(8,128)} %x_ref.7), custom_call_target="tpu_custom_call" | custom-call | flops 196608 | bytes 1179648 | tf_op jit(solution)/shard_map/pallas_call | solution.py:86
  2.0 1.3 %shard_map.122.low_ref = bf16[96,2048]{1,0:T(8,128)(2,1)S(1)} custom-call(f32[96,4096]{1,0:T(8,128)} %x_ref.7), custom_call_target="tpu_custom_call" | custom-call | flops 196608 | bytes 1179648 | tf_op jit(solution)/shard_map/pallas_call | solution.py:86
  3.3 0.0 copy-done.1
  3.3 0.0 copy-done.3
  3.3 0.0 copy-done.2
  3.3 0.0 copy-done.7
  3.3 0.0 copy-done.6
  3.3 0.0 copy-done.5
  3.3 0.0 copy-done.4
  3.4 0.0 copy-start
  3.4 0.0 copy-start.8
  3.4 3.2 %shard_map.124 = (f32[8,1,128]{2,1,0:T(1,128)}, bf16[5,128,128]{2,1,0:T(8,128)(2,1)}, bf16[15,128,128]{2,1,0:T(8,128)(2,1)}, f32[32,128]{1,0:T(8,128)S(1)}, f32[32,128]{1,0:T(8,128)S(1)}, /*index=5*/s32[2,160]{1,0:T(2,128)S(1)}) custom-call(f32[96,4096]{1,0:T(8,128)} %x_ref.7, bf16[96,2048]{1,0:T(8,128)(2,1)S(1)} %shard_map.122.low_ref, ...), custom_call_target="tpu_custom_call" | custom-call | flops 32768000 | bytes 1572864 | tf_op jit(solution)/shard_map/pallas_call | solution.py:385
  6.6 1.3 %collective-permute-start.3 = (bf16[15,128,128]{2,1,0:T(8,128)(2,1)}, bf16[15,128,128]{2,1,0:T(8,128)(2,1)S(1)}, u32[]{:S(2)}, u32[]{:S(2)}) collective-permute-start(bf16[15,128,128]{2,1,0:T(8,128)(2,1)} %get-tuple-element.18), channel_id=1, source_target_pairs={{1,0},{2,1},{3,2},{4,3},{5,4},{6,5},{7,6},{9,8},{10,9},{11,10},{12... | collective-permute-start | bytes 1474568 | tf_op jit(solution)/shard_map/ppermute | solution.py:39
  7.9 1.3 %collective-permute-start.1 = (bf16[96,2048]{1,0:T(8,128)(2,1)S(1)}, bf16[96,2048]{1,0:T(8,128)(2,1)S(1)}, u32[]{:S(2)}, u32[]{:S(2)}) collective-permute-start(bf16[96,2048]{1,0:T(8,128)(2,1)S(1)} %shard_map.122.low_ref), channel_id=1, source_target_pairs={{1,0},{2,1},{3,2},{4,3},{5,4},{6,5},{7,6},{8,7},{9,8},{10,9},{11,1... | collective-permute-start | bytes 1179656 | tf_op jit(solution)/shard_map/ppermute | solution.py:33
  9.2 6.2 %collective-permute-start = (bf16[96,2048]{1,0:T(8,128)(2,1)S(1)}, bf16[96,2048]{1,0:T(8,128)(2,1)S(1)}, u32[]{:S(2)}, u32[]{:S(2)}) collective-permute-start(bf16[96,2048]{1,0:T(8,128)(2,1)S(1)} %shard_map.123.high_ref), channel_id=1, source_target_pairs={{0,1},{1,2},{2,3},{3,4},{4,5},{5,6},{6,7},{7,8},{8,9},{9,10},{10,1... | collective-permute-start | bytes 1179656 | tf_op jit(solution)/shard_map/ppermute | solution.py:33
  15.3 1.3 %collective-permute-start.2 = (bf16[5,128,128]{2,1,0:T(8,128)(2,1)}, bf16[5,128,128]{2,1,0:T(8,128)(2,1)S(1)}, u32[]{:S(2)}, u32[]{:S(2)}) collective-permute-start(bf16[5,128,128]{2,1,0:T(8,128)(2,1)} %get-tuple-element.17), channel_id=1, source_target_pairs={{1,0},{2,1},{3,2},{4,3},{5,4},{6,5},{7,6},{9,8},{10,9},{11,10},{12... | collective-permute-start | bytes 491528 | tf_op jit(solution)/shard_map/ppermute | solution.py:39
  16.6 9.3 %all-to-all-start = ((f32[8,1,128]{2,1,0:T(1,128)}), f32[8,1,128]{2,1,0:T(1,128)S(1)}, u32[]{:S(2)}, u32[]{:S(2)}) async-start(f32[8,1,128]{2,1,0:T(1,128)} %get-tuple-element.15), calls=%async_computation | async-start | bytes 8192 | tf_op jit(solution)/shard_map/all_to_all | solution.py:422
  25.9 0.0 copy-done
  25.9 0.0 copy-done.8
  25.9 4.0 %shard_map.125.base_ref = f32[96,4096]{1,0:T(8,128)} custom-call(f32[96,4096]{1,0:T(8,128)} %x_ref.7, bf16[96,2048]{1,0:T(8,128)(2,1)S(1)} %shard_map.122.low_ref, bf16[96,2048]{1,0:T(8,128)(2,1)S(1)} %shard_map.123.high_ref, f32[32,128]{1,0:T(8,128)S(1)} %get-tuple-element.13.light_ref, f32[32,128]{1,0:T(8,128)S(1)} %get-tuple-element.14.wet_ref, ...), custom_call_target="tpu_custom_call" | custom-call | flops 122880000 | bytes 3145728 | tf_op jit(solution)/shard_map/pallas_call | solution.py:426
  30.0 13.4 %all-to-all-done.received_ref = f32[8,1,128]{2,1,0:T(1,128)S(1)} async-done(((f32[8,1,128]{2,1,0:T(1,128)}), f32[8,1,128]{2,1,0:T(1,128)S(1)}, u32[]{:S(2)}, u32[]{:S(2)}) %all-to-all-start) | async-done | bytes 4128 | tf_op jit(solution)/shard_map/all_to_all | solution.py:422
  43.4 0.0 collective-permute-done.1.right_ref
  43.4 0.0 collective-permute-done.left_ref
  43.4 8.8 %shard_map.126 = (f32[96,4224]{1,0:T(8,128)S(1)}, bf16[20,96,128]{2,1,0:T(8,128)(2,1)S(1)}, s32[1,128]{1,0:T(1,128)S(1)}, f32[1,128]{1,0:T(1,128)}) custom-call(s32[2,160]{1,0:T(2,128)S(1)} %get-tuple-element.12.index_ref, bf16[160,128,128]{2,1,0:T(8,128)(2,1)} %tiles_ref.3, bf16[96,2048]{1,0:T(8,128)(2,1)S(1)} %shard_map.122.low_ref, ...), custom_call_target="tpu_custom_call" | custom-call | flops 503316480 | bytes 5242880 | tf_op jit(solution)/shard_map/pallas_call | solution.py:453
  52.2 0.0 collective-permute-done.2.lead_ref
  52.2 0.0 collective-permute-done.3.rest_ref
  52.2 2.3 %shard_map.127 = f32[96,4096]{1,0:T(8,128)} custom-call(s32[1,128]{1,0:T(1,128)S(1)} %get-tuple-element.16.slot_ref, bf16[5,128,128]{2,1,0:T(8,128)(2,1)S(1)} %collective-permute-done.2.lead_ref, bf16[15,128,128]{2,1,0:T(8,128)(2,1)S(1)} %collective-permute-done.3.rest_ref, bf16[20,96,128]{2,1,0:T(8,128)(2,1)S(1)} %get-tuple-element.19.picked_ref, ...), custom_call_target="tpu_custom_call" | custom-call | flops 62914560 | bytes 3145728 | tf_op jit(solution)/shard_map/pallas_call | solution.py:477
Async XLA Ops:
  0.6 2.7 %copy-start.1 = (f32[64,16]{0,1:T(8,128)S(1)}, f32[64,16]{0,1:T(8,128)}, u32[]{:S(2)}) copy-start(f32[64,16]{0,1:T(8,128)} %param.19) | copy-start | bytes 12292
  0.6 2.7 %copy-start.3 = (f32[64]{0:T(128)S(1)}, f32[64]{0:T(128)}, u32[]{:S(2)}) copy-start(f32[64]{0:T(128)} %param.18) | copy-start | bytes 772
  0.7 2.7 %copy-start.2 = (f32[16]{0:T(128)S(1)}, f32[16]{0:T(128)}, u32[]{:S(2)}) copy-start(f32[16]{0:T(128)} %param.17) | copy-start | bytes 196
  0.7 2.7 %copy-start.7 = (s32[128]{0:T(128)S(1)}, s32[128]{0:T(128)}, u32[]{:S(2)}) copy-start(s32[128]{0:T(128)} %param.16) | copy-start | bytes 1540
  0.7 2.7 %copy-start.6 = (s32[128]{0:T(128)S(1)}, s32[128]{0:T(128)}, u32[]{:S(2)}) copy-start(s32[128]{0:T(128)} %param.15) | copy-start | bytes 1540
  0.7 2.7 %copy-start.5 = (s32[160]{0:T(256)S(1)}, s32[160]{0:T(256)}, u32[]{:S(2)}) copy-start(s32[160]{0:T(256)} %param.13) | copy-start | bytes 1924
  0.7 2.7 %copy-start.4 = (s32[160]{0:T(256)S(1)}, s32[160]{0:T(256)}, u32[]{:S(2)}) copy-start(s32[160]{0:T(256)} %param.12) | copy-start | bytes 1924
  3.4 22.6 %copy-start = (f32[64,64]{1,0:T(8,128)S(1)}, f32[64,64]{1,0:T(8,128)}, u32[]{:S(2)}) copy-start(f32[64,64]{1,0:T(8,128)} %prefer_ref.1) | copy-start | bytes 49156
  3.4 22.6 %copy-start.8 = (f32[64]{0:T(128)S(1)}, f32[64]{0:T(128)}, u32[]{:S(2)}) copy-start(f32[64]{0:T(128)} %param.21) | copy-start | bytes 772
  6.6 45.7 %collective-permute-start.3 = (bf16[15,128,128]{2,1,0:T(8,128)(2,1)}, bf16[15,128,128]{2,1,0:T(8,128)(2,1)S(1)}, u32[]{:S(2)}, u32[]{:S(2)}) collective-permute-start(bf16[15,128,128]{2,1,0:T(8,128)(2,1)} %get-tuple-element.18), channel_id=1, source_target_pairs={{1,0},{2,1},{3,2},{4,3},{5,4},{6,5},{7,6},{9,8},{10,9},{11,10},{12... | collective-permute-start | bytes 1474568 | tf_op jit(solution)/shard_map/ppermute | solution.py:39
  7.9 35.5 %collective-permute-start.1 = (bf16[96,2048]{1,0:T(8,128)(2,1)S(1)}, bf16[96,2048]{1,0:T(8,128)(2,1)S(1)}, u32[]{:S(2)}, u32[]{:S(2)}) collective-permute-start(bf16[96,2048]{1,0:T(8,128)(2,1)S(1)} %shard_map.122.low_ref), channel_id=1, source_target_pairs={{1,0},{2,1},{3,2},{4,3},{5,4},{6,5},{7,6},{8,7},{9,8},{10,9},{11,1... | collective-permute-start | bytes 1179656 | tf_op jit(solution)/shard_map/ppermute | solution.py:33
  9.2 34.2 %collective-permute-start = (bf16[96,2048]{1,0:T(8,128)(2,1)S(1)}, bf16[96,2048]{1,0:T(8,128)(2,1)S(1)}, u32[]{:S(2)}, u32[]{:S(2)}) collective-permute-start(bf16[96,2048]{1,0:T(8,128)(2,1)S(1)} %shard_map.123.high_ref), channel_id=1, source_target_pairs={{0,1},{1,2},{2,3},{3,4},{4,5},{5,6},{6,7},{7,8},{8,9},{9,10},{10,1... | collective-permute-start | bytes 1179656 | tf_op jit(solution)/shard_map/ppermute | solution.py:33
  15.3 36.9 %collective-permute-start.2 = (bf16[5,128,128]{2,1,0:T(8,128)(2,1)}, bf16[5,128,128]{2,1,0:T(8,128)(2,1)S(1)}, u32[]{:S(2)}, u32[]{:S(2)}) collective-permute-start(bf16[5,128,128]{2,1,0:T(8,128)(2,1)} %get-tuple-element.17), channel_id=1, source_target_pairs={{1,0},{2,1},{3,2},{4,3},{5,4},{6,5},{7,6},{9,8},{10,9},{11,10},{12... | collective-permute-start | bytes 491528 | tf_op jit(solution)/shard_map/ppermute | solution.py:39
  16.6 26.7 %all-to-all-start = ((f32[8,1,128]{2,1,0:T(1,128)}), f32[8,1,128]{2,1,0:T(1,128)S(1)}, u32[]{:S(2)}, u32[]{:S(2)}) async-start(f32[8,1,128]{2,1,0:T(1,128)} %get-tuple-element.15), calls=%async_computation | async-start | bytes 8192 | tf_op jit(solution)/shard_map/all_to_all | solution.py:422

commit v4 on v3

--- a/solution.py
+++ b/solution.py
@@ -64,24 +64,23 @@
 
 def round_kernel(start, x_ref, out_ref, held_ref, sems):
     pieces = sems.shape[0]
-    width = out_ref.shape[1] // pieces
+    rows, width = out_ref.shape[0] // pieces, out_ref.shape[1]
 
     def load(k):
+        at = pl.ds(k * rows, rows)
         return pltpu.make_async_copy(
-            x_ref.at[:, pl.ds(start + k * width, width)],
-            held_ref.at[:, pl.ds(k * width, width)],
-            sems.at[k],
+            x_ref.at[at, pl.ds(start, width)], held_ref.at[at], sems.at[k]
         )
 
     for k in range(pieces):
         load(k).start()
     for k in range(pieces):
         load(k).wait()
-        at = slice(k * width, (k + 1) * width)
-        out_ref[:, at] = held_ref[:, at].astype(BF16)
-
-
-def rounded(x, start, width, pieces=4):
+        at = slice(k * rows, (k + 1) * rows)
+        out_ref[at, :] = held_ref[at, :].astype(BF16)
+
+
+def rounded(x, start, width, pieces=3):
     rows = x.shape[0]
     return pl.pallas_call(
         functools.partial(round_kernel, start),
@@ -124,13 +123,12 @@
 def produce_kernel(
     x_ref, low_ref, high_ref, level_ref, owner_ref, half_ref, rate_ref, uptake_ref,
     rows_ref, cols_ref, tiles_ref,
-    send_ref, lead_ref, rest_ref, light_ref, wet_ref, index_ref, sums_ref, made_ref, held_ref,
+    send_ref, more_ref, light_ref, wet_ref, index_ref, sums_ref, made_ref, held_ref,
     few_ref, more_sem, few_sem,
 ):
     few = pltpu.make_async_copy(x_ref.at[pl.ds(0, NUT)], few_ref, few_sem)
     few.start()
-    lead = lead_ref.shape[0]
-    spill = lead + rest_ref.shape[0]
+    spill = more_ref.shape[0]
     pack = pltpu.make_async_copy(tiles_ref.at[pl.ds(0, spill)], held_ref, more_sem)
     pack.start()
     cells = x_ref.shape[1]
@@ -162,12 +160,8 @@
             made_ref[row : row + 1, :] = taken[:, s * LANES : (s + 1) * LANES]
 
     pack.wait()
-    packs = [
-        pltpu.make_async_copy(held_ref.at[pl.ds(0, lead)], lead_ref, more_sem),
-        pltpu.make_async_copy(held_ref.at[pl.ds(lead, spill - lead)], rest_ref, few_sem),
-    ]
-    for pack in packs:
-        pack.start()
+    pack = pltpu.make_async_copy(held_ref, more_ref, more_sem)
+    pack.start()
 
     mine = iota((blocks, columns), 1) // per_block == iota((blocks, columns), 0)
     spread = iota((columns, LANES), 0) % per_block == iota((columns, LANES), 1) // LEV
@@ -197,8 +191,7 @@
     index = jnp.where(lane < share + spill, rows, cols)
     for o in range(devices):
         send_ref[o] = jnp.where(lane < share, sorted_sums[o : o + 1, :], index)
-    for pack in packs:
-        pack.wait()
+    pack.wait()
 
 
 def ecosystem_kernel(
@@ -337,7 +330,7 @@
     lax.fori_loop(0, pieces, piece, 0)
 
 
-def last_kernel(slot_ref, lead_ref, rest_ref, picked_ref, mid_ref, out_ref, total_ref, out_sem):
+def last_kernel(slot_ref, tiles_ref, picked_ref, mid_ref, out_ref, total_ref, out_sem):
     cells = out_ref.shape[1]
     blocks = cells // LANES
 
@@ -346,16 +339,14 @@
         pltpu.make_async_copy(total_ref.at[:, at], out_ref.at[:, at], out_sem).start()
         return carry
 
-    total_ref[...] = mid_ref[...]
-    done, before = 0, 0
-    for ref in (lead_ref, rest_ref):
-        head = slot_ref[0, before]
+    count = tiles_ref.shape[0]
+    done = 0
+    for begin in (0, count // 2):
+        head = slot_ref[0, begin]
         lax.fori_loop(done, head, store, 0)
         done = jnp.maximum(done, head)
-        for j in range(ref.shape[0]):
-            t = before + j
-            total_ref[:, block_at(slot_ref[0, t])] += rows_dot(picked_ref[t], ref[j])
-        before += ref.shape[0]
+        for t in range(begin, count if begin else count // 2):
+            total_ref[:, block_at(slot_ref[0, t])] += rows_dot(picked_ref[t], tiles_ref[t])
     lax.fori_loop(done, blocks, store, 0)
     pltpu.make_async_copy(total_ref.at[:, pl.ds(0, cells)], out_ref, out_sem).wait()
 
@@ -381,19 +372,17 @@
 
     share = level_counts.shape[0] // devices
     blocks = cells // block
-    lead = spill // 4
-    send, spilled_lead, spilled_rest, light, wet, index = pl.pallas_call(
+    send, spilled, light, wet, index = pl.pallas_call(
         produce_kernel,
         out_shape=(
             jax.ShapeDtypeStruct((devices, 1, LANES), F32),
-            pltpu.HBM((lead, block, block), BF16),
-            pltpu.HBM((spill - lead, block, block), BF16),
+            pltpu.HBM((spill, block, block), BF16),
             jax.ShapeDtypeStruct((blocks, LANES), F32),
             jax.ShapeDtypeStruct((blocks, LANES), F32),
             jax.ShapeDtypeStruct((2, tile_total), jnp.int32),
         ),
         in_specs=[HBM_SPEC] + [VMEM_SPEC] * 9 + [HBM_SPEC],
-        out_specs=(VMEM_SPEC, HBM_SPEC, HBM_SPEC) + (VMEM_SPEC,) * 3,
+        out_specs=(VMEM_SPEC, HBM_SPEC) + (VMEM_SPEC,) * 3,
         scratch_shapes=[
             pltpu.VMEM((blocks, LANES), F32),
             pltpu.VMEM((blocks, LANES), F32),
@@ -421,8 +410,7 @@
     )
     received = lax.all_to_all(send, "dev", split_axis=0, concat_axis=0, tiled=True)
 
-    lead_tiles = group_shift(spilled_lead, -1)
-    rest_tiles = group_shift(spilled_rest, -1)
+    more_tiles = group_shift(spilled, -1)
     base = pl.pallas_call(
         ecosystem_kernel,
         out_shape=pltpu.HBM((channels, cells), F32),
@@ -474,20 +462,21 @@
             flops=tile_total * work, bytes_accessed=tile_values.size * 2, transcendentals=0
         ),
     )(index, tiles, low, high, left, right, in_hbm(base), received)
-    updated = pl.pallas_call(
+    updated, _ = pl.pallas_call(
         last_kernel,
-        out_shape=jax.ShapeDtypeStruct((channels, cells), F32),
-        in_specs=[smem] + [VMEM_SPEC] * 4,
-        out_specs=HBM_SPEC,
-        scratch_shapes=[
-            pltpu.VMEM((channels, cells + LANES), F32),
-            pltpu.SemaphoreType.DMA,
-        ],
+        out_shape=(
+            jax.ShapeDtypeStruct((channels, cells), F32),
+            jax.ShapeDtypeStruct((channels, cells + LANES), F32),
+        ),
+        in_specs=[smem] + [VMEM_SPEC] * 3,
+        out_specs=(HBM_SPEC, VMEM_SPEC),
+        scratch_shapes=[pltpu.SemaphoreType.DMA],
+        input_output_aliases={3: 1},
         compiler_params=pltpu.CompilerParams(vmem_limit_bytes=6 << 20),
         cost_estimate=pl.CostEstimate(
             flops=spill * work, bytes_accessed=channels * cells * 8, transcendentals=0
         ),
-    )(slots, lead_tiles, rest_tiles, picked, mid)
+    )(slots, more_tiles, picked, mid)
     return updated, made.reshape(-1)
 
 

time: 54.9 us -> 54.1 us (0.985)
  starting transfers between devices: 19.3 us -> 18 us
  waiting for transfers between devices: 13.4 us -> 14.7 us
  Pallas kernels: 20.9 us -> 20.2 us
    ppermute x2 -> x1, starting transfers between devices: 2.58 us -> 1.29 us  [group_shift(): return lax.ppermute(x, 'dev', pairs)]
    all_to_all x1, waiting for transfers between devices: 13.4 us -> 14.7 us  [per_device(): lax.all_to_all(send, 'dev', split_axis=0, concat_axis=0, tiled=True)]
  transfers between devices with their start and end apart: 5 -> 4, of which waited for: 1 -> 1; matrix products, arithmetic and copies ran while one was open for 0% -> 0% of each run, Pallas kernels for 24% -> 24%
where the time goes in v4:
time: 54.1 us; the launch traced here: 53.8 us
  Pallas kernels  20.2 us (37%)
  starting transfers between devices  18 us (33%)
  waiting for transfers between devices  14.7 us (27%)
  between operations  0.84 us (2%)
    all_to_all x1, waiting for transfers between devices, per_device(): lax.all_to_all(send, 'dev', split_axis=0, concat_axis=0, tiled=True)  14.7 us
    all_to_all x1, starting transfers between devices, per_device(): lax.all_to_all(send, 'dev', split_axis=0, concat_axis=0, tiled=True)  9.27 us
    pallas_call x1, Pallas kernels, per_device(): pl.pallas_call(local_kernel, out_shape=(jax.ShapeDtypeStruct((channels, c...  8.82 us
    ppermute x2, starting transfers between devices, chain_shift(): return lax.ppermute(x, CHAIN, pairs)  7.47 us
    pallas_call x1, Pallas kernels, per_device(): pl.pallas_call(ecosystem_kernel, out_shape=pltpu.HBM((channels, cells), F...  4.03 us
    pallas_call x1, Pallas kernels, per_device(): pl.pallas_call(produce_kernel, out_shape=(jax.ShapeDtypeStruct((devices,...  2.82 us
    pallas_call x2, Pallas kernels, rounded(): pl.pallas_call(functools.partial(round_kernel, start), out_shape=jax.Shap...  2.34 us
    pallas_call x1, Pallas kernels, per_device(): pl.pallas_call(last_kernel, out_shape=(jax.ShapeDtypeStruct((channels, ce...  2.17 us
  transfers between devices with their start and end apart: 4, of which 1 were waited for; matrix products, arithmetic and copies ran while one was open for 0% of the time, Pallas kernels for 24%

profile of v4, /device:TPU:0, one launch (start us, length us, event | category | flops | bytes accessed | tf_op | source)
XLA Modules:
  0.0 53.8 jit_solution(14196444829626934531)
XLA Ops:
  0.6 0.0 copy-start.1
  0.6 0.0 copy-start.3
  0.7 0.0 copy-start.2
  0.7 0.0 copy-start.7
  0.7 0.0 copy-start.6
  0.7 0.0 copy-start.5
  0.7 0.0 copy-start.4
  0.7 1.2 %shard_map.123.high_ref = bf16[96,2048]{1,0:T(8,128)(2,1)S(1)} custom-call(f32[96,4096]{1,0:T(8,128)} %x_ref.7), custom_call_target="tpu_custom_call" | custom-call | flops 196608 | bytes 1179648 | tf_op jit(solution)/shard_map/pallas_call | solution.py:85
  1.9 1.2 %shard_map.122.low_ref = bf16[96,2048]{1,0:T(8,128)(2,1)S(1)} custom-call(f32[96,4096]{1,0:T(8,128)} %x_ref.7), custom_call_target="tpu_custom_call" | custom-call | flops 196608 | bytes 1179648 | tf_op jit(solution)/shard_map/pallas_call | solution.py:85
  3.1 0.0 copy-done.1
  3.1 0.0 copy-done.3
  3.1 0.0 copy-done.2
  3.1 0.0 copy-done.7
  3.1 0.0 copy-done.6
  3.1 0.0 copy-done.5
  3.1 0.0 copy-done.4
  3.1 0.0 copy-start
  3.1 0.0 copy-start.8
  3.2 2.8 %shard_map.124 = (f32[8,1,128]{2,1,0:T(1,128)}, bf16[20,128,128]{2,1,0:T(8,128)(2,1)}, f32[32,128]{1,0:T(8,128)S(1)}, f32[32,128]{1,0:T(8,128)S(1)}, s32[2,160]{1,0:T(2,128)S(1)}) custom-call(f32[96,4096]{1,0:T(8,128)} %x_ref.7, bf16[96,2048]{1,0:T(8,128)(2,1)S(1)} %shard_map.122.low_ref, bf16[96,2048]{1,0:T(8,128)(2,1)S(1)} %shard_map.123.high_ref, ...), custom_call_target="tpu_custom_call" | custom-call | flops 32768000 | bytes 1572864 | tf_op jit(solution)/shard_map/pallas_call | solution.py:375
  6.0 1.3 %collective-permute-start.2 = (bf16[20,128,128]{2,1,0:T(8,128)(2,1)}, bf16[20,128,128]{2,1,0:T(8,128)(2,1)S(1)}, u32[]{:S(2)}, u32[]{:S(2)}) collective-permute-start(bf16[20,128,128]{2,1,0:T(8,128)(2,1)} %get-tuple-element.17), channel_id=1, source_target_pairs={{1,0},{2,1},{3,2},{4,3},{5,4},{6,5},{7,6},{9,8},{10,9},{11,10},{12... | collective-permute-start | bytes 1966088 | tf_op jit(solution)/shard_map/ppermute | solution.py:39
  7.3 1.3 %collective-permute-start.1 = (bf16[96,2048]{1,0:T(8,128)(2,1)S(1)}, bf16[96,2048]{1,0:T(8,128)(2,1)S(1)}, u32[]{:S(2)}, u32[]{:S(2)}) collective-permute-start(bf16[96,2048]{1,0:T(8,128)(2,1)S(1)} %shard_map.122.low_ref), channel_id=1, source_target_pairs={{1,0},{2,1},{3,2},{4,3},{5,4},{6,5},{7,6},{8,7},{9,8},{10,9},{11,1... | collective-permute-start | bytes 1179656 | tf_op jit(solution)/shard_map/ppermute | solution.py:33
  8.6 6.2 %collective-permute-start = (bf16[96,2048]{1,0:T(8,128)(2,1)S(1)}, bf16[96,2048]{1,0:T(8,128)(2,1)S(1)}, u32[]{:S(2)}, u32[]{:S(2)}) collective-permute-start(bf16[96,2048]{1,0:T(8,128)(2,1)S(1)} %shard_map.123.high_ref), channel_id=1, source_target_pairs={{0,1},{1,2},{2,3},{3,4},{4,5},{5,6},{6,7},{7,8},{8,9},{9,10},{10,1... | collective-permute-start | bytes 1179656 | tf_op jit(solution)/shard_map/ppermute | solution.py:33
  14.8 9.3 %all-to-all-start = ((f32[8,1,128]{2,1,0:T(1,128)}), f32[8,1,128]{2,1,0:T(1,128)S(1)}, u32[]{:S(2)}, u32[]{:S(2)}) async-start(f32[8,1,128]{2,1,0:T(1,128)} %get-tuple-element.15), calls=%async_computation | async-start | bytes 8192 | tf_op jit(solution)/shard_map/all_to_all | solution.py:411
  24.0 0.0 copy-done
  24.0 0.0 copy-done.8
  24.0 4.0 %shard_map.125.base_ref = f32[96,4096]{1,0:T(8,128)} custom-call(f32[96,4096]{1,0:T(8,128)} %x_ref.7, bf16[96,2048]{1,0:T(8,128)(2,1)S(1)} %shard_map.122.low_ref, bf16[96,2048]{1,0:T(8,128)(2,1)S(1)} %shard_map.123.high_ref, f32[32,128]{1,0:T(8,128)S(1)} %get-tuple-element.13.light_ref, f32[32,128]{1,0:T(8,128)S(1)} %get-tuple-element.14.wet_ref, ...), custom_call_target="tpu_custom_call" | custom-call | flops 122880000 | bytes 3145728 | tf_op jit(solution)/shard_map/pallas_call | solution.py:414
  28.1 14.7 %all-to-all-done.received_ref = f32[8,1,128]{2,1,0:T(1,128)S(1)} async-done(((f32[8,1,128]{2,1,0:T(1,128)}), f32[8,1,128]{2,1,0:T(1,128)S(1)}, u32[]{:S(2)}, u32[]{:S(2)}) %all-to-all-start) | async-done | bytes 4128 | tf_op jit(solution)/shard_map/all_to_all | solution.py:411
  42.8 0.0 collective-permute-done.1.right_ref
  42.8 0.0 collective-permute-done.left_ref
  42.8 8.8 %shard_map.126 = (f32[96,4224]{1,0:T(8,128)S(1)}, bf16[20,96,128]{2,1,0:T(8,128)(2,1)S(1)}, s32[1,128]{1,0:T(1,128)S(1)}, f32[1,128]{1,0:T(1,128)}) custom-call(s32[2,160]{1,0:T(2,128)S(1)} %get-tuple-element.12.index_ref, bf16[160,128,128]{2,1,0:T(8,128)(2,1)} %tiles_ref.3, bf16[96,2048]{1,0:T(8,128)(2,1)S(1)} %shard_map.122.low_ref, ...), custom_call_target="tpu_custom_call" | custom-call | flops 503316480 | bytes 5242880 | tf_op jit(solution)/shard_map/pallas_call | solution.py:441
  51.6 0.0 collective-permute-done.2.tiles_ref
  51.6 2.2 %shard_map.127 = (f32[96,4096]{1,0:T(8,128)}, f32[96,4224]{1,0:T(8,128)S(1)}) custom-call(s32[1,128]{1,0:T(1,128)S(1)} %get-tuple-element.16.slot_ref, bf16[20,128,128]{2,1,0:T(8,128)(2,1)S(1)} %collective-permute-done.2.tiles_ref, bf16[20,96,128]{2,1,0:T(8,128)(2,1)S(1)} %get-tuple-element.18.picked_ref, ...), custom_call_target="tpu_custom_call", output_to_operand_aliasing={{1}: (3, {})} | custom-call | flops 62914560 | bytes 3145728 | tf_op jit(solution)/shard_map/pallas_call | solution.py:465
Async XLA Ops:
  0.6 2.4 %copy-start.1 = (f32[64,16]{0,1:T(8,128)S(1)}, f32[64,16]{0,1:T(8,128)}, u32[]{:S(2)}) copy-start(f32[64,16]{0,1:T(8,128)} %param.19) | copy-start | bytes 12292
  0.6 2.4 %copy-start.3 = (f32[64]{0:T(128)S(1)}, f32[64]{0:T(128)}, u32[]{:S(2)}) copy-start(f32[64]{0:T(128)} %param.18) | copy-start | bytes 772
  0.7 2.4 %copy-start.2 = (f32[16]{0:T(128)S(1)}, f32[16]{0:T(128)}, u32[]{:S(2)}) copy-start(f32[16]{0:T(128)} %param.17) | copy-start | bytes 196
  0.7 2.4 %copy-start.7 = (s32[128]{0:T(128)S(1)}, s32[128]{0:T(128)}, u32[]{:S(2)}) copy-start(s32[128]{0:T(128)} %param.16) | copy-start | bytes 1540
  0.7 2.4 %copy-start.6 = (s32[128]{0:T(128)S(1)}, s32[128]{0:T(128)}, u32[]{:S(2)}) copy-start(s32[128]{0:T(128)} %param.15) | copy-start | bytes 1540
  0.7 2.4 %copy-start.5 = (s32[160]{0:T(256)S(1)}, s32[160]{0:T(256)}, u32[]{:S(2)}) copy-start(s32[160]{0:T(256)} %param.13) | copy-start | bytes 1924
  0.7 2.4 %copy-start.4 = (s32[160]{0:T(256)S(1)}, s32[160]{0:T(256)}, u32[]{:S(2)}) copy-start(s32[160]{0:T(256)} %param.12) | copy-start | bytes 1924
  3.1 20.9 %copy-start = (f32[64,64]{1,0:T(8,128)S(1)}, f32[64,64]{1,0:T(8,128)}, u32[]{:S(2)}) copy-start(f32[64,64]{1,0:T(8,128)} %prefer_ref.1) | copy-start | bytes 49156
  3.1 20.9 %copy-start.8 = (f32[64]{0:T(128)S(1)}, f32[64]{0:T(128)}, u32[]{:S(2)}) copy-start(f32[64]{0:T(128)} %param.21) | copy-start | bytes 772
  6.0 45.7 %collective-permute-start.2 = (bf16[20,128,128]{2,1,0:T(8,128)(2,1)}, bf16[20,128,128]{2,1,0:T(8,128)(2,1)S(1)}, u32[]{:S(2)}, u32[]{:S(2)}) collective-permute-start(bf16[20,128,128]{2,1,0:T(8,128)(2,1)} %get-tuple-element.17), channel_id=1, source_target_pairs={{1,0},{2,1},{3,2},{4,3},{5,4},{6,5},{7,6},{9,8},{10,9},{11,10},{12... | collective-permute-start | bytes 1966088 | tf_op jit(solution)/shard_map/ppermute | solution.py:39
  7.3 35.5 %collective-permute-start.1 = (bf16[96,2048]{1,0:T(8,128)(2,1)S(1)}, bf16[96,2048]{1,0:T(8,128)(2,1)S(1)}, u32[]{:S(2)}, u32[]{:S(2)}) collective-permute-start(bf16[96,2048]{1,0:T(8,128)(2,1)S(1)} %shard_map.122.low_ref), channel_id=1, source_target_pairs={{1,0},{2,1},{3,2},{4,3},{5,4},{6,5},{7,6},{8,7},{9,8},{10,9},{11,1... | collective-permute-start | bytes 1179656 | tf_op jit(solution)/shard_map/ppermute | solution.py:33
  8.6 34.2 %collective-permute-start = (bf16[96,2048]{1,0:T(8,128)(2,1)S(1)}, bf16[96,2048]{1,0:T(8,128)(2,1)S(1)}, u32[]{:S(2)}, u32[]{:S(2)}) collective-permute-start(bf16[96,2048]{1,0:T(8,128)(2,1)S(1)} %shard_map.123.high_ref), channel_id=1, source_target_pairs={{0,1},{1,2},{2,3},{3,4},{4,5},{5,6},{6,7},{7,8},{8,9},{9,10},{10,1... | collective-permute-start | bytes 1179656 | tf_op jit(solution)/shard_map/ppermute | solution.py:33
  14.8 28.0 %all-to-all-start = ((f32[8,1,128]{2,1,0:T(1,128)}), f32[8,1,128]{2,1,0:T(1,128)S(1)}, u32[]{:S(2)}, u32[]{:S(2)}) async-start(f32[8,1,128]{2,1,0:T(1,128)} %get-tuple-element.15), calls=%async_computation | async-start | bytes 8192 | tf_op jit(solution)/shard_map/all_to_all | solution.py:411

commit v5 on v4

--- a/solution.py
+++ b/solution.py
@@ -30,6 +30,12 @@
 def chain_shift(x, step):
     count = lax.axis_size(CHAIN)
     pairs = [(i, i + step) for i in range(count) if 0 <= i + step < count]
+    return lax.ppermute(x, CHAIN, pairs)
+
+
+def down_shift(x, near):
+    count, group = lax.axis_size(CHAIN), lax.axis_size("dev")
+    pairs = [(i, i - 1) for i in range(1, count) if (i % group == 1) == near]
     return lax.ppermute(x, CHAIN, pairs)
 
 
@@ -113,6 +119,20 @@
     )
 
 
+def halves(a):
+    top = a.astype(BF16)
+    return top, (a - top.astype(F32)).astype(BF16)
+
+
+def left_parts(a):
+    top, rest = halves(a)
+    return jnp.concatenate([v.astype(F32) for v in (top, rest, top)], axis=1).astype(BF16)
+
+
+def right_parts(top, rest):
+    return jnp.concatenate([top, top, rest], axis=0)
+
+
 def plankton_sent(low_ref, high_ref, c, width):
     half = low_ref.shape[1]
     start = c * width
@@ -124,10 +144,17 @@
     x_ref, low_ref, high_ref, level_ref, owner_ref, half_ref, rate_ref, uptake_ref,
     rows_ref, cols_ref, tiles_ref,
     send_ref, more_ref, light_ref, wet_ref, index_ref, sums_ref, made_ref, held_ref,
-    few_ref, more_sem, few_sem,
+    few_ref, more_sem, few_sems,
 ):
-    few = pltpu.make_async_copy(x_ref.at[pl.ds(0, NUT)], few_ref, few_sem)
-    few.start()
+    pieces = few_sems.shape[0]
+    piece = x_ref.shape[1] // pieces
+
+    def load(k):
+        at = (pl.ds(0, NUT + PLK), pl.ds(k * piece, piece))
+        return pltpu.make_async_copy(x_ref.at[at], few_ref.at[at], few_sems.at[k])
+
+    for k in range(pieces):
+        load(k).start()
     spill = more_ref.shape[0]
     pack = pltpu.make_async_copy(tiles_ref.at[pl.ds(0, spill)], held_ref, more_sem)
     pack.start()
@@ -144,13 +171,17 @@
     share = columns // devices
 
     half = upright(half_ref)
-    weight = jnp.concatenate(
-        [uptake_ref[...] * rate_ref[...], jnp.ones((NUT, PLK), F32)], axis=0
-    ).astype(BF16)
-    few.wait()
+    weight = left_parts(
+        jnp.concatenate([uptake_ref[...] * rate_ref[...], jnp.ones((NUT, PLK), F32)], axis=0)
+    )
     for c in range(cells // SPAN):
-        both = dot(weight, plankton_sent(low_ref, high_ref, c, SPAN))
-        nutrient = few_ref[:, c * SPAN : (c + 1) * SPAN]
+        if c * SPAN % piece == 0:
+            load(c * SPAN // piece).wait()
+        at = slice(c * SPAN, (c + 1) * SPAN)
+        top = plankton_sent(low_ref, high_ref, c, SPAN)
+        rest = (few_ref[NUT:, at] - top.astype(F32)).astype(BF16)
+        both = dot(weight, right_parts(top, rest))
+        nutrient = few_ref[:NUT, at]
         monod = nutrient / (nutrient + half)
         total = both[NUT : NUT + 1]
         taken = jnp.sum(monod * both[:NUT], axis=0, keepdims=True)
@@ -213,16 +244,11 @@
     rate = upright(rate_ref)
     most = upright(graze_ref)
     prefer = prefer_ref[...]
-    uptake_b = uptake_ref[...].T.astype(BF16)
+    uptake_b = left_parts(uptake_ref[...].T)
     quarter = (iota((NUT, PLK), 1) // (PLK // NUT) == iota((NUT, PLK), 0)).astype(F32)
-    first = jnp.concatenate([prefer, uptake_ref[...] * rate_ref[...]], axis=0).astype(BF16)
-    second = jnp.concatenate(
-        [
-            jnp.concatenate([prefer.T, jnp.zeros((PLK, 2 * PLK), F32)], axis=1),
-            jnp.concatenate([jnp.zeros((NUT, PLK), F32), quarter, quarter], axis=1),
-        ],
-        axis=0,
-    ).astype(BF16)
+    quarter_b = jnp.concatenate([quarter, quarter], axis=1).astype(BF16)
+    first = left_parts(jnp.concatenate([prefer, uptake_ref[...] * rate_ref[...]], axis=0))
+    second = left_parts(prefer.T)
     span = CHUNK // LANES
 
     def row_of(ref, c):
@@ -238,18 +264,17 @@
         detritus = held_ref[NUT + PLK :, at]
         sun = row_of(light_ref, c)
         mask = row_of(wet_ref, c)
-        both = dot(first, plankton_b)
+        rest = (plankton - plankton_b.astype(F32)).astype(BF16)
+        both = dot(first, right_parts(plankton_b, rest))
         food, drawn = both[:PLK], both[PLK:]
         monod = nutrient / (nutrient + half)
-        limitation = dot(uptake_b, monod.astype(BF16))
+        limitation = dot(uptake_b, right_parts(*halves(monod)))
         growth = rate * sun * plankton * limitation
         graze = most * plankton / (1.0 + food)
         eaten = graze * food
         waste = (1.0 - EFFICIENCY) * eaten + MORTALITY * plankton
-        waste_high = waste.astype(BF16)
-        waste_low = (waste - waste_high.astype(F32)).astype(BF16)
-        both = dot(second, jnp.concatenate([graze.astype(BF16), waste_high, waste_low], axis=0))
-        lost, fallen = both[:PLK], both[PLK:]
+        lost = dot(second, right_parts(*halves(graze)))
+        fallen = dot(quarter_b, jnp.concatenate(halves(waste), axis=0))
         d_plankton = growth - plankton * lost + EFFICIENCY * eaten - MORTALITY * plankton
         d_nutrient = REMINERAL * detritus - monod * sun * drawn
         d_detritus = fallen - REMINERAL * detritus
@@ -277,7 +302,7 @@
     return (lax.axis_index("grp") * lax.axis_size("dev") + lax.axis_index("dev")) * blocks
 
 
-def local_kernel(index_ref, tiles_ref, low_ref, high_ref, left_ref, right_ref, base_ref,
+def local_kernel(index_ref, tiles_ref, low_ref, high_ref, left_ref, right_ref, near_ref, base_ref,
                  received_ref, out_ref, picked_ref, slot_ref, made_ref,
                  reach_ref, held_ref, vector_ref, far_ref, sems, base_sem, far_sem):
     cells = base_ref.shape[1]
@@ -311,7 +336,7 @@
     for k in range(1, pieces):
         load(k).start()
     for k, ref in enumerate((low_ref, high_ref, right_ref, left_ref)):
-        reach_ref[:, part_of(k)] = ref[...]
+        reach_ref[:, part_of(k)] = ref[...] + near_ref[...] if k == 2 else ref[...]
     move.wait()
     for t in range(spill):
         picked_ref[t] = reach_ref[:, block_at(far_ref[0, share + spill + t])]
@@ -341,11 +366,12 @@
 
     count = tiles_ref.shape[0]
     done = 0
-    for begin in (0, count // 2):
+    step = pl.cdiv(count, 4)
+    for begin in range(0, count, step):
         head = slot_ref[0, begin]
         lax.fori_loop(done, head, store, 0)
         done = jnp.maximum(done, head)
-        for t in range(begin, count if begin else count // 2):
+        for t in range(begin, min(begin + step, count)):
             total_ref[:, block_at(slot_ref[0, t])] += rows_dot(picked_ref[t], tiles_ref[t])
     lax.fori_loop(done, blocks, store, 0)
     pltpu.make_async_copy(total_ref.at[:, pl.ds(0, cells)], out_ref, out_sem).wait()
@@ -368,7 +394,8 @@
     high = rounded(source, half, half)
     low = rounded(source, 0, half)
     left = chain_shift(high, 1)
-    right = chain_shift(low, -1)
+    right = down_shift(low, False)
+    near = down_shift(low, True)
 
     share = level_counts.shape[0] // devices
     blocks = cells // block
@@ -387,9 +414,9 @@
             pltpu.VMEM((blocks, LANES), F32),
             pltpu.VMEM((blocks, LANES), F32),
             pltpu.VMEM((spill, block, block), BF16),
-            pltpu.VMEM((NUT, cells), F32),
+            pltpu.VMEM((NUT + PLK, cells), F32),
             pltpu.SemaphoreType.DMA,
-            pltpu.SemaphoreType.DMA,
+            pltpu.SemaphoreType.DMA((4,)),
         ],
         compiler_params=pltpu.CompilerParams(vmem_limit_bytes=4 << 20),
         cost_estimate=pl.CostEstimate(
@@ -446,7 +473,7 @@
             jax.ShapeDtypeStruct((1, LANES), jnp.int32),
             jax.ShapeDtypeStruct((1, devices * share), F32),
         ),
-        in_specs=[smem, HBM_SPEC] + [VMEM_SPEC] * 4 + [HBM_SPEC, VMEM_SPEC],
+        in_specs=[smem, HBM_SPEC] + [VMEM_SPEC] * 5 + [HBM_SPEC, VMEM_SPEC],
         out_specs=(VMEM_SPEC,) * 4,
         scratch_shapes=[
             pltpu.VMEM((channels, 4 * half), BF16),
@@ -461,7 +488,7 @@
         cost_estimate=pl.CostEstimate(
             flops=tile_total * work, bytes_accessed=tile_values.size * 2, transcendentals=0
         ),
-    )(index, tiles, low, high, left, right, in_hbm(base), received)
+    )(index, tiles, low, high, left, right, near, in_hbm(base), received)
     updated, _ = pl.pallas_call(
         last_kernel,
         out_shape=(

time: 54.1 us -> 54.9 us (1.015)
  Pallas kernels: 20.2 us -> 22.1 us
  starting transfers between devices: 18 us -> 17.1 us
    ppermute x0 -> x2, starting transfers between devices: none -> 1.98 us  [down_shift(): return lax.ppermute(x, CHAIN, pairs)]
    ppermute x2 -> x1, starting transfers between devices: 7.47 us -> 5.55 us  [chain_shift(): return lax.ppermute(x, CHAIN, pairs)]
    pallas_call x1, Pallas kernels: 4.03 us -> 5.3 us  [per_device(): pl.pallas_call(ecosystem_kernel, out_shape=pltpu.HBM((channels, cells), F...]
    all_to_all x1, starting transfers between devices: 9.27 us -> 8.29 us  [per_device(): lax.all_to_all(send, 'dev', split_axis=0, concat_axis=0, tiled=True)]
  transfers between devices with their start and end apart: 4 -> 5, of which waited for: 1 -> 1; matrix products, arithmetic and copies ran while one was open for 0% -> 0% of each run, Pallas kernels for 24% -> 26%
where the time goes in v5:
time: 54.9 us; the launch traced here: 54.6 us
  Pallas kernels  22.1 us (40%)
  starting transfers between devices  17.1 us (31%)
  waiting for transfers between devices  14.5 us (26%)
  between operations  0.85 us (2%)
    all_to_all x1, waiting for transfers between devices, per_device(): lax.all_to_all(send, 'dev', split_axis=0, concat_axis=0, tiled=True)  14.5 us
    pallas_call x1, Pallas kernels, per_device(): pl.pallas_call(local_kernel, out_shape=(jax.ShapeDtypeStruct((channels, c...  8.82 us
    all_to_all x1, starting transfers between devices, per_device(): lax.all_to_all(send, 'dev', split_axis=0, concat_axis=0, tiled=True)  8.29 us
    ppermute x1, starting transfers between devices, chain_shift(): return lax.ppermute(x, CHAIN, pairs)  5.55 us
    pallas_call x1, Pallas kernels, per_device(): pl.pallas_call(ecosystem_kernel, out_shape=pltpu.HBM((channels, cells), F...  5.3 us
    pallas_call x1, Pallas kernels, per_device(): pl.pallas_call(produce_kernel, out_shape=(jax.ShapeDtypeStruct((devices,...  3.22 us
    pallas_call x1, Pallas kernels, per_device(): pl.pallas_call(last_kernel, out_shape=(jax.ShapeDtypeStruct((channels, ce...  2.4 us
    pallas_call x2, Pallas kernels, rounded(): pl.pallas_call(functools.partial(round_kernel, start), out_shape=jax.Shap...  2.34 us
  transfers between devices with their start and end apart: 5, of which 1 were waited for; matrix products, arithmetic and copies ran while one was open for 0% of the time, Pallas kernels for 26%

profile of v5, /device:TPU:0, one launch (start us, length us, event | category | flops | bytes accessed | tf_op | source)
XLA Modules:
  0.0 54.6 jit_solution(1254149327766907659)
XLA Ops:
  0.6 0.0 copy-start.1
  0.6 0.0 copy-start.3
  0.7 0.0 copy-start.2
  0.7 0.0 copy-start.7
  0.7 0.0 copy-start.6
  0.7 0.0 copy-start.5
  0.7 0.0 copy-start.4
  0.7 1.2 %shard_map.122.low_ref = bf16[96,2048]{1,0:T(8,128)(2,1)S(1)} custom-call(f32[96,4096]{1,0:T(8,128)} %x_ref.7), custom_call_target="tpu_custom_call" | custom-call | flops 196608 | bytes 1179648 | tf_op jit(solution)/shard_map/pallas_call | solution.py:91
  1.9 1.2 %shard_map.123.high_ref = bf16[96,2048]{1,0:T(8,128)(2,1)S(1)} custom-call(f32[96,4096]{1,0:T(8,128)} %x_ref.7), custom_call_target="tpu_custom_call" | custom-call | flops 196608 | bytes 1179648 | tf_op jit(solution)/shard_map/pallas_call | solution.py:91
  3.1 0.0 copy-done.1
  3.1 0.0 copy-done.3
  3.1 0.0 copy-done.2
  3.1 0.0 copy-done.7
  3.1 0.0 copy-done.6
  3.1 0.0 copy-done.5
  3.1 0.0 copy-done.4
  3.1 0.0 copy-start
  3.1 0.0 copy-start.8
  3.2 3.2 %shard_map.124 = (f32[8,1,128]{2,1,0:T(1,128)}, bf16[20,128,128]{2,1,0:T(8,128)(2,1)}, f32[32,128]{1,0:T(8,128)S(1)}, f32[32,128]{1,0:T(8,128)S(1)}, s32[2,160]{1,0:T(2,128)S(1)}) custom-call(f32[96,4096]{1,0:T(8,128)} %x_ref.7, bf16[96,2048]{1,0:T(8,128)(2,1)S(1)} %shard_map.122.low_ref, bf16[96,2048]{1,0:T(8,128)(2,1)S(1)} %shard_map.123.high_ref, ...), custom_call_target="tpu_custom_call" | custom-call | flops 32768000 | bytes 1572864 | tf_op jit(solution)/shard_map/pallas_call | solution.py:402
  6.4 1.3 %collective-permute-start.3 = (bf16[20,128,128]{2,1,0:T(8,128)(2,1)}, bf16[20,128,128]{2,1,0:T(8,128)(2,1)S(1)}, u32[]{:S(2)}, u32[]{:S(2)}) collective-permute-start(bf16[20,128,128]{2,1,0:T(8,128)(2,1)} %get-tuple-element.17), channel_id=1, source_target_pairs={{1,0},{2,1},{3,2},{4,3},{5,4},{6,5},{7,6},{9,8},{10,9},{11,10},{12... | collective-permute-start | bytes 1966088 | tf_op jit(solution)/shard_map/ppermute | solution.py:45
  7.7 5.6 %collective-permute-start = (bf16[96,2048]{1,0:T(8,128)(2,1)S(1)}, bf16[96,2048]{1,0:T(8,128)(2,1)S(1)}, u32[]{:S(2)}, u32[]{:S(2)}) collective-permute-start(bf16[96,2048]{1,0:T(8,128)(2,1)S(1)} %shard_map.123.high_ref), channel_id=1, source_target_pairs={{0,1},{1,2},{2,3},{3,4},{4,5},{5,6},{6,7},{7,8},{8,9},{9,10},{10,1... | collective-permute-start | bytes 1179656 | tf_op jit(solution)/shard_map/ppermute | solution.py:33
  13.2 1.3 %collective-permute-start.2 = (bf16[96,2048]{1,0:T(8,128)(2,1)S(1)}, bf16[96,2048]{1,0:T(8,128)(2,1)S(1)}, u32[]{:S(2)}, u32[]{:S(2)}) collective-permute-start(bf16[96,2048]{1,0:T(8,128)(2,1)S(1)} %shard_map.122.low_ref), channel_id=1, source_target_pairs={{1,0},{9,8},{17,16},{25,24}} | collective-permute-start | bytes 1179656 | tf_op jit(solution)/shard_map/ppermute | solution.py:39
  14.5 0.7 %collective-permute-start.1 = (bf16[96,2048]{1,0:T(8,128)(2,1)S(1)}, bf16[96,2048]{1,0:T(8,128)(2,1)S(1)}, u32[]{:S(2)}, u32[]{:S(2)}) collective-permute-start(bf16[96,2048]{1,0:T(8,128)(2,1)S(1)} %shard_map.122.low_ref), channel_id=1, source_target_pairs={{2,1},{3,2},{4,3},{5,4},{6,5},{7,6},{8,7},{10,9},{11,10},{12,11},{... | collective-permute-start | bytes 1179656 | tf_op jit(solution)/shard_map/ppermute | solution.py:39
  15.2 8.3 %all-to-all-start = ((f32[8,1,128]{2,1,0:T(1,128)}), f32[8,1,128]{2,1,0:T(1,128)S(1)}, u32[]{:S(2)}, u32[]{:S(2)}) async-start(f32[8,1,128]{2,1,0:T(1,128)} %get-tuple-element.15), calls=%async_computation | async-start | bytes 8192 | tf_op jit(solution)/shard_map/all_to_all | solution.py:438
  23.5 0.0 copy-done
  23.5 0.0 copy-done.8
  23.5 5.3 %shard_map.125.base_ref = f32[96,4096]{1,0:T(8,128)} custom-call(f32[96,4096]{1,0:T(8,128)} %x_ref.7, bf16[96,2048]{1,0:T(8,128)(2,1)S(1)} %shard_map.122.low_ref, bf16[96,2048]{1,0:T(8,128)(2,1)S(1)} %shard_map.123.high_ref, f32[32,128]{1,0:T(8,128)S(1)} %get-tuple-element.13.light_ref, f32[32,128]{1,0:T(8,128)S(1)} %get-tuple-element.14.wet_ref, ...), custom_call_target="tpu_custom_call" | custom-call | flops 122880000 | bytes 3145728 | tf_op jit(solution)/shard_map/pallas_call | solution.py:441
  28.8 14.5 %all-to-all-done.received_ref = f32[8,1,128]{2,1,0:T(1,128)S(1)} async-done(((f32[8,1,128]{2,1,0:T(1,128)}), f32[8,1,128]{2,1,0:T(1,128)S(1)}, u32[]{:S(2)}, u32[]{:S(2)}) %all-to-all-start) | async-done | bytes 4128 | tf_op jit(solution)/shard_map/all_to_all | solution.py:438
  43.3 0.0 collective-permute-done.left_ref
  43.3 0.0 collective-permute-done.2.near_ref
  43.3 0.0 collective-permute-done.1.right_ref
  43.3 8.8 %shard_map.126 = (f32[96,4224]{1,0:T(8,128)S(1)}, bf16[20,96,128]{2,1,0:T(8,128)(2,1)S(1)}, s32[1,128]{1,0:T(1,128)S(1)}, f32[1,128]{1,0:T(1,128)}) custom-call(s32[2,160]{1,0:T(2,128)S(1)} %get-tuple-element.12.index_ref, bf16[160,128,128]{2,1,0:T(8,128)(2,1)} %tiles_ref.3, bf16[96,2048]{1,0:T(8,128)(2,1)S(1)} %shard_map.122.low_ref, ...), custom_call_target="tpu_custom_call" | custom-call | flops 503316480 | bytes 5242880 | tf_op jit(solution)/shard_map/pallas_call | solution.py:468
  52.1 0.0 collective-permute-done.3.tiles_ref
  52.1 2.4 %shard_map.127 = (f32[96,4096]{1,0:T(8,128)}, f32[96,4224]{1,0:T(8,128)S(1)}) custom-call(s32[1,128]{1,0:T(1,128)S(1)} %get-tuple-element.16.slot_ref, bf16[20,128,128]{2,1,0:T(8,128)(2,1)S(1)} %collective-permute-done.3.tiles_ref, bf16[20,96,128]{2,1,0:T(8,128)(2,1)S(1)} %get-tuple-element.18.picked_ref, ...), custom_call_target="tpu_custom_call", output_to_operand_aliasing={{1}: (3, {})} | custom-call | flops 62914560 | bytes 3145728 | tf_op jit(solution)/shard_map/pallas_call | solution.py:492
Async XLA Ops:
  0.6 2.4 %copy-start.1 = (f32[64,16]{0,1:T(8,128)S(1)}, f32[64,16]{0,1:T(8,128)}, u32[]{:S(2)}) copy-start(f32[64,16]{0,1:T(8,128)} %param.19) | copy-start | bytes 12292
  0.6 2.4 %copy-start.3 = (f32[64]{0:T(128)S(1)}, f32[64]{0:T(128)}, u32[]{:S(2)}) copy-start(f32[64]{0:T(128)} %param.18) | copy-start | bytes 772
  0.7 2.4 %copy-start.2 = (f32[16]{0:T(128)S(1)}, f32[16]{0:T(128)}, u32[]{:S(2)}) copy-start(f32[16]{0:T(128)} %param.17) | copy-start | bytes 196
  0.7 2.4 %copy-start.7 = (s32[128]{0:T(128)S(1)}, s32[128]{0:T(128)}, u32[]{:S(2)}) copy-start(s32[128]{0:T(128)} %param.16) | copy-start | bytes 1540
  0.7 2.4 %copy-start.6 = (s32[128]{0:T(128)S(1)}, s32[128]{0:T(128)}, u32[]{:S(2)}) copy-start(s32[128]{0:T(128)} %param.15) | copy-start | bytes 1540
  0.7 2.4 %copy-start.5 = (s32[160]{0:T(256)S(1)}, s32[160]{0:T(256)}, u32[]{:S(2)}) copy-start(s32[160]{0:T(256)} %param.13) | copy-start | bytes 1924
  0.7 2.4 %copy-start.4 = (s32[160]{0:T(256)S(1)}, s32[160]{0:T(256)}, u32[]{:S(2)}) copy-start(s32[160]{0:T(256)} %param.12) | copy-start | bytes 1924
  3.1 20.4 %copy-start = (f32[64,64]{1,0:T(8,128)S(1)}, f32[64,64]{1,0:T(8,128)}, u32[]{:S(2)}) copy-start(f32[64,64]{1,0:T(8,128)} %prefer_ref.1) | copy-start | bytes 49156
  3.1 20.4 %copy-start.8 = (f32[64]{0:T(128)S(1)}, f32[64]{0:T(128)}, u32[]{:S(2)}) copy-start(f32[64]{0:T(128)} %param.21) | copy-start | bytes 772
  6.4 45.8 %collective-permute-start.3 = (bf16[20,128,128]{2,1,0:T(8,128)(2,1)}, bf16[20,128,128]{2,1,0:T(8,128)(2,1)S(1)}, u32[]{:S(2)}, u32[]{:S(2)}) collective-permute-start(bf16[20,128,128]{2,1,0:T(8,128)(2,1)} %get-tuple-element.17), channel_id=1, source_target_pairs={{1,0},{2,1},{3,2},{4,3},{5,4},{6,5},{7,6},{9,8},{10,9},{11,10},{12... | collective-permute-start | bytes 1966088 | tf_op jit(solution)/shard_map/ppermute | solution.py:45
  7.7 35.6 %collective-permute-start = (bf16[96,2048]{1,0:T(8,128)(2,1)S(1)}, bf16[96,2048]{1,0:T(8,128)(2,1)S(1)}, u32[]{:S(2)}, u32[]{:S(2)}) collective-permute-start(bf16[96,2048]{1,0:T(8,128)(2,1)S(1)} %shard_map.123.high_ref), channel_id=1, source_target_pairs={{0,1},{1,2},{2,3},{3,4},{4,5},{5,6},{6,7},{7,8},{8,9},{9,10},{10,1... | collective-permute-start | bytes 1179656 | tf_op jit(solution)/shard_map/ppermute | solution.py:33
  13.2 30.1 %collective-permute-start.2 = (bf16[96,2048]{1,0:T(8,128)(2,1)S(1)}, bf16[96,2048]{1,0:T(8,128)(2,1)S(1)}, u32[]{:S(2)}, u32[]{:S(2)}) collective-permute-start(bf16[96,2048]{1,0:T(8,128)(2,1)S(1)} %shard_map.122.low_ref), channel_id=1, source_target_pairs={{1,0},{9,8},{17,16},{25,24}} | collective-permute-start | bytes 1179656 | tf_op jit(solution)/shard_map/ppermute | solution.py:39
  14.5 28.8 %collective-permute-start.1 = (bf16[96,2048]{1,0:T(8,128)(2,1)S(1)}, bf16[96,2048]{1,0:T(8,128)(2,1)S(1)}, u32[]{:S(2)}, u32[]{:S(2)}) collective-permute-start(bf16[96,2048]{1,0:T(8,128)(2,1)S(1)} %shard_map.122.low_ref), channel_id=1, source_target_pairs={{2,1},{3,2},{4,3},{5,4},{6,5},{7,6},{8,7},{10,9},{11,10},{12,11},{... | collective-permute-start | bytes 1179656 | tf_op jit(solution)/shard_map/ppermute | solution.py:39
  15.2 28.1 %all-to-all-start = ((f32[8,1,128]{2,1,0:T(1,128)}), f32[8,1,128]{2,1,0:T(1,128)S(1)}, u32[]{:S(2)}, u32[]{:S(2)}) async-start(f32[8,1,128]{2,1,0:T(1,128)} %get-tuple-element.15), calls=%async_computation | async-start | bytes 8192 | tf_op jit(solution)/shard_map/all_to_all | solution.py:438

commit v6 on v5

--- a/solution.py
+++ b/solution.py
@@ -35,7 +35,7 @@
 
 def down_shift(x, near):
     count, group = lax.axis_size(CHAIN), lax.axis_size("dev")
-    pairs = [(i, i - 1) for i in range(1, count) if (i % group == 1) == near]
+    pairs = [(i, i - 1) for i in range(1, count) if (i % group <= 1) == near]
     return lax.ppermute(x, CHAIN, pairs)
 
 
@@ -366,12 +366,11 @@
 
     count = tiles_ref.shape[0]
     done = 0
-    step = pl.cdiv(count, 4)
-    for begin in range(0, count, step):
+    for begin in (0, count // 2):
         head = slot_ref[0, begin]
         lax.fori_loop(done, head, store, 0)
         done = jnp.maximum(done, head)
-        for t in range(begin, min(begin + step, count)):
+        for t in range(begin, count if begin else count // 2):
             total_ref[:, block_at(slot_ref[0, t])] += rows_dot(picked_ref[t], tiles_ref[t])
     lax.fori_loop(done, blocks, store, 0)
     pltpu.make_async_copy(total_ref.at[:, pl.ds(0, cells)], out_ref, out_sem).wait()

time: 54.9 us -> 54.6 us (level)
  no operation moved by 1% of the time
where the time goes in v6:
time: 54.6 us; the launch traced here: 54.3 us
  Pallas kernels  21.9 us (40%)
  starting transfers between devices  17.1 us (31%)
  waiting for transfers between devices  14.5 us (27%)
  between operations  0.85 us (2%)
    all_to_all x1, waiting for transfers between devices, per_device(): lax.all_to_all(send, 'dev', split_axis=0, concat_axis=0, tiled=True)  14.5 us
    pallas_call x1, Pallas kernels, per_device(): pl.pallas_call(local_kernel, out_shape=(jax.ShapeDtypeStruct((channels, c...  8.82 us
    all_to_all x1, starting transfers between devices, per_device(): lax.all_to_all(send, 'dev', split_axis=0, concat_axis=0, tiled=True)  8.29 us
    ppermute x1, starting transfers between devices, chain_shift(): return lax.ppermute(x, CHAIN, pairs)  5.55 us
    pallas_call x1, Pallas kernels, per_device(): pl.pallas_call(ecosystem_kernel, out_shape=pltpu.HBM((channels, cells), F...  5.3 us
    pallas_call x1, Pallas kernels, per_device(): pl.pallas_call(produce_kernel, out_shape=(jax.ShapeDtypeStruct((devices,...  3.22 us
    pallas_call x2, Pallas kernels, rounded(): pl.pallas_call(functools.partial(round_kernel, start), out_shape=jax.Shap...  2.34 us
    pallas_call x1, Pallas kernels, per_device(): pl.pallas_call(last_kernel, out_shape=(jax.ShapeDtypeStruct((channels, ce...  2.17 us
  transfers between devices with their start and end apart: 5, of which 1 were waited for; matrix products, arithmetic and copies ran while one was open for 0% of the time, Pallas kernels for 26%

profile of v6, /device:TPU:0, one launch (start us, length us, event | category | flops | bytes accessed | tf_op | source)
XLA Modules:
  0.0 54.3 jit_solution(1957425657256722837)
XLA Ops:
  0.6 0.0 copy-start.1
  0.6 0.0 copy-start.3
  0.7 0.0 copy-start.2
  0.7 0.0 copy-start.7
  0.7 0.0 copy-start.6
  0.7 0.0 copy-start.5
  0.7 0.0 copy-start.4
  0.7 1.2 %shard_map.122.low_ref = bf16[96,2048]{1,0:T(8,128)(2,1)S(1)} custom-call(f32[96,4096]{1,0:T(8,128)} %x_ref.7), custom_call_target="tpu_custom_call" | custom-call | flops 196608 | bytes 1179648 | tf_op jit(solution)/shard_map/pallas_call | solution.py:91
  1.9 1.2 %shard_map.123.high_ref = bf16[96,2048]{1,0:T(8,128)(2,1)S(1)} custom-call(f32[96,4096]{1,0:T(8,128)} %x_ref.7), custom_call_target="tpu_custom_call" | custom-call | flops 196608 | bytes 1179648 | tf_op jit(solution)/shard_map/pallas_call | solution.py:91
  3.1 0.0 copy-done.1
  3.1 0.0 copy-done.3
  3.1 0.0 copy-done.2
  3.1 0.0 copy-done.7
  3.1 0.0 copy-done.6
  3.1 0.0 copy-done.5
  3.1 0.0 copy-done.4
  3.1 0.0 copy-start
  3.1 0.0 copy-start.8
  3.2 3.2 %shard_map.124 = (f32[8,1,128]{2,1,0:T(1,128)}, bf16[20,128,128]{2,1,0:T(8,128)(2,1)}, f32[32,128]{1,0:T(8,128)S(1)}, f32[32,128]{1,0:T(8,128)S(1)}, s32[2,160]{1,0:T(2,128)S(1)}) custom-call(f32[96,4096]{1,0:T(8,128)} %x_ref.7, bf16[96,2048]{1,0:T(8,128)(2,1)S(1)} %shard_map.122.low_ref, bf16[96,2048]{1,0:T(8,128)(2,1)S(1)} %shard_map.123.high_ref, ...), custom_call_target="tpu_custom_call" | custom-call | flops 32768000 | bytes 1572864 | tf_op jit(solution)/shard_map/pallas_call | solution.py:401
  6.4 1.3 %collective-permute-start.3 = (bf16[20,128,128]{2,1,0:T(8,128)(2,1)}, bf16[20,128,128]{2,1,0:T(8,128)(2,1)S(1)}, u32[]{:S(2)}, u32[]{:S(2)}) collective-permute-start(bf16[20,128,128]{2,1,0:T(8,128)(2,1)} %get-tuple-element.17), channel_id=1, source_target_pairs={{1,0},{2,1},{3,2},{4,3},{5,4},{6,5},{7,6},{9,8},{10,9},{11,10},{12... | collective-permute-start | bytes 1966088 | tf_op jit(solution)/shard_map/ppermute | solution.py:45
  7.7 5.6 %collective-permute-start = (bf16[96,2048]{1,0:T(8,128)(2,1)S(1)}, bf16[96,2048]{1,0:T(8,128)(2,1)S(1)}, u32[]{:S(2)}, u32[]{:S(2)}) collective-permute-start(bf16[96,2048]{1,0:T(8,128)(2,1)S(1)} %shard_map.123.high_ref), channel_id=1, source_target_pairs={{0,1},{1,2},{2,3},{3,4},{4,5},{5,6},{6,7},{7,8},{8,9},{9,10},{10,1... | collective-permute-start | bytes 1179656 | tf_op jit(solution)/shard_map/ppermute | solution.py:33
  13.2 1.3 %collective-permute-start.2 = (bf16[96,2048]{1,0:T(8,128)(2,1)S(1)}, bf16[96,2048]{1,0:T(8,128)(2,1)S(1)}, u32[]{:S(2)}, u32[]{:S(2)}) collective-permute-start(bf16[96,2048]{1,0:T(8,128)(2,1)S(1)} %shard_map.122.low_ref), channel_id=1, source_target_pairs={{1,0},{8,7},{9,8},{16,15},{17,16},{24,23},{25,24}} | collective-permute-start | bytes 1179656 | tf_op jit(solution)/shard_map/ppermute | solution.py:39
  14.5 0.7 %collective-permute-start.1 = (bf16[96,2048]{1,0:T(8,128)(2,1)S(1)}, bf16[96,2048]{1,0:T(8,128)(2,1)S(1)}, u32[]{:S(2)}, u32[]{:S(2)}) collective-permute-start(bf16[96,2048]{1,0:T(8,128)(2,1)S(1)} %shard_map.122.low_ref), channel_id=1, source_target_pairs={{2,1},{3,2},{4,3},{5,4},{6,5},{7,6},{10,9},{11,10},{12,11},{13,12}... | collective-permute-start | bytes 1179656 | tf_op jit(solution)/shard_map/ppermute | solution.py:39
  15.2 8.3 %all-to-all-start = ((f32[8,1,128]{2,1,0:T(1,128)}), f32[8,1,128]{2,1,0:T(1,128)S(1)}, u32[]{:S(2)}, u32[]{:S(2)}) async-start(f32[8,1,128]{2,1,0:T(1,128)} %get-tuple-element.15), calls=%async_computation | async-start | bytes 8192 | tf_op jit(solution)/shard_map/all_to_all | solution.py:437
  23.5 0.0 copy-done
  23.5 0.0 copy-done.8
  23.5 5.3 %shard_map.125.base_ref = f32[96,4096]{1,0:T(8,128)} custom-call(f32[96,4096]{1,0:T(8,128)} %x_ref.7, bf16[96,2048]{1,0:T(8,128)(2,1)S(1)} %shard_map.122.low_ref, bf16[96,2048]{1,0:T(8,128)(2,1)S(1)} %shard_map.123.high_ref, f32[32,128]{1,0:T(8,128)S(1)} %get-tuple-element.13.light_ref, f32[32,128]{1,0:T(8,128)S(1)} %get-tuple-element.14.wet_ref, ...), custom_call_target="tpu_custom_call" | custom-call | flops 122880000 | bytes 3145728 | tf_op jit(solution)/shard_map/pallas_call | solution.py:440
  28.8 14.5 %all-to-all-done.received_ref = f32[8,1,128]{2,1,0:T(1,128)S(1)} async-done(((f32[8,1,128]{2,1,0:T(1,128)}), f32[8,1,128]{2,1,0:T(1,128)S(1)}, u32[]{:S(2)}, u32[]{:S(2)}) %all-to-all-start) | async-done | bytes 4128 | tf_op jit(solution)/shard_map/all_to_all | solution.py:437
  43.3 0.0 collective-permute-done.left_ref
  43.3 0.0 collective-permute-done.2.near_ref
  43.3 0.0 collective-permute-done.1.right_ref
  43.3 8.8 %shard_map.126 = (f32[96,4224]{1,0:T(8,128)S(1)}, bf16[20,96,128]{2,1,0:T(8,128)(2,1)S(1)}, s32[1,128]{1,0:T(1,128)S(1)}, f32[1,128]{1,0:T(1,128)}) custom-call(s32[2,160]{1,0:T(2,128)S(1)} %get-tuple-element.12.index_ref, bf16[160,128,128]{2,1,0:T(8,128)(2,1)} %tiles_ref.3, bf16[96,2048]{1,0:T(8,128)(2,1)S(1)} %shard_map.122.low_ref, ...), custom_call_target="tpu_custom_call" | custom-call | flops 503316480 | bytes 5242880 | tf_op jit(solution)/shard_map/pallas_call | solution.py:467
  52.1 0.0 collective-permute-done.3.tiles_ref
  52.1 2.2 %shard_map.127 = (f32[96,4096]{1,0:T(8,128)}, f32[96,4224]{1,0:T(8,128)S(1)}) custom-call(s32[1,128]{1,0:T(1,128)S(1)} %get-tuple-element.16.slot_ref, bf16[20,128,128]{2,1,0:T(8,128)(2,1)S(1)} %collective-permute-done.3.tiles_ref, bf16[20,96,128]{2,1,0:T(8,128)(2,1)S(1)} %get-tuple-element.18.picked_ref, ...), custom_call_target="tpu_custom_call", output_to_operand_aliasing={{1}: (3, {})} | custom-call | flops 62914560 | bytes 3145728 | tf_op jit(solution)/shard_map/pallas_call | solution.py:491
Async XLA Ops:
  0.6 2.4 %copy-start.1 = (f32[64,16]{0,1:T(8,128)S(1)}, f32[64,16]{0,1:T(8,128)}, u32[]{:S(2)}) copy-start(f32[64,16]{0,1:T(8,128)} %param.19) | copy-start | bytes 12292
  0.6 2.4 %copy-start.3 = (f32[64]{0:T(128)S(1)}, f32[64]{0:T(128)}, u32[]{:S(2)}) copy-start(f32[64]{0:T(128)} %param.18) | copy-start | bytes 772
  0.7 2.4 %copy-start.2 = (f32[16]{0:T(128)S(1)}, f32[16]{0:T(128)}, u32[]{:S(2)}) copy-start(f32[16]{0:T(128)} %param.17) | copy-start | bytes 196
  0.7 2.4 %copy-start.7 = (s32[128]{0:T(128)S(1)}, s32[128]{0:T(128)}, u32[]{:S(2)}) copy-start(s32[128]{0:T(128)} %param.16) | copy-start | bytes 1540
  0.7 2.4 %copy-start.6 = (s32[128]{0:T(128)S(1)}, s32[128]{0:T(128)}, u32[]{:S(2)}) copy-start(s32[128]{0:T(128)} %param.15) | copy-start | bytes 1540
  0.7 2.4 %copy-start.5 = (s32[160]{0:T(256)S(1)}, s32[160]{0:T(256)}, u32[]{:S(2)}) copy-start(s32[160]{0:T(256)} %param.13) | copy-start | bytes 1924
  0.7 2.4 %copy-start.4 = (s32[160]{0:T(256)S(1)}, s32[160]{0:T(256)}, u32[]{:S(2)}) copy-start(s32[160]{0:T(256)} %param.12) | copy-start | bytes 1924
  3.1 20.4 %copy-start = (f32[64,64]{1,0:T(8,128)S(1)}, f32[64,64]{1,0:T(8,128)}, u32[]{:S(2)}) copy-start(f32[64,64]{1,0:T(8,128)} %prefer_ref.1) | copy-start | bytes 49156
  3.1 20.4 %copy-start.8 = (f32[64]{0:T(128)S(1)}, f32[64]{0:T(128)}, u32[]{:S(2)}) copy-start(f32[64]{0:T(128)} %param.21) | copy-start | bytes 772
  6.4 45.8 %collective-permute-start.3 = (bf16[20,128,128]{2,1,0:T(8,128)(2,1)}, bf16[20,128,128]{2,1,0:T(8,128)(2,1)S(1)}, u32[]{:S(2)}, u32[]{:S(2)}) collective-permute-start(bf16[20,128,128]{2,1,0:T(8,128)(2,1)} %get-tuple-element.17), channel_id=1, source_target_pairs={{1,0},{2,1},{3,2},{4,3},{5,4},{6,5},{7,6},{9,8},{10,9},{11,10},{12... | collective-permute-start | bytes 1966088 | tf_op jit(solution)/shard_map/ppermute | solution.py:45
  7.7 35.6 %collective-permute-start = (bf16[96,2048]{1,0:T(8,128)(2,1)S(1)}, bf16[96,2048]{1,0:T(8,128)(2,1)S(1)}, u32[]{:S(2)}, u32[]{:S(2)}) collective-permute-start(bf16[96,2048]{1,0:T(8,128)(2,1)S(1)} %shard_map.123.high_ref), channel_id=1, source_target_pairs={{0,1},{1,2},{2,3},{3,4},{4,5},{5,6},{6,7},{7,8},{8,9},{9,10},{10,1... | collective-permute-start | bytes 1179656 | tf_op jit(solution)/shard_map/ppermute | solution.py:33
  13.2 30.1 %collective-permute-start.2 = (bf16[96,2048]{1,0:T(8,128)(2,1)S(1)}, bf16[96,2048]{1,0:T(8,128)(2,1)S(1)}, u32[]{:S(2)}, u32[]{:S(2)}) collective-permute-start(bf16[96,2048]{1,0:T(8,128)(2,1)S(1)} %shard_map.122.low_ref), channel_id=1, source_target_pairs={{1,0},{8,7},{9,8},{16,15},{17,16},{24,23},{25,24}} | collective-permute-start | bytes 1179656 | tf_op jit(solution)/shard_map/ppermute | solution.py:39
  14.5 28.8 %collective-permute-start.1 = (bf16[96,2048]{1,0:T(8,128)(2,1)S(1)}, bf16[96,2048]{1,0:T(8,128)(2,1)S(1)}, u32[]{:S(2)}, u32[]{:S(2)}) collective-permute-start(bf16[96,2048]{1,0:T(8,128)(2,1)S(1)} %shard_map.122.low_ref), channel_id=1, source_target_pairs={{2,1},{3,2},{4,3},{5,4},{6,5},{7,6},{10,9},{11,10},{12,11},{13,12}... | collective-permute-start | bytes 1179656 | tf_op jit(solution)/shard_map/ppermute | solution.py:39
  15.2 28.1 %all-to-all-start = ((f32[8,1,128]{2,1,0:T(1,128)}), f32[8,1,128]{2,1,0:T(1,128)S(1)}, u32[]{:S(2)}, u32[]{:S(2)}) async-start(f32[8,1,128]{2,1,0:T(1,128)} %get-tuple-element.15), calls=%async_computation | async-start | bytes 8192 | tf_op jit(solution)/shard_map/all_to_all | solution.py:437
